TPU v7x, 256 devices: a whole 4x4x8 slice. The times are simulated.
256 devices in a mesh: dp: 32 (over y, x, core), filter: 8 (over z).
Axes of the slice: x: 4, y: 4, z: 8, core: 2. Of those that a mesh axis runs over, the one named last changes fastest.
Arguments:
- inputs: bfloat16 [32, 48, 24, 1024], P('dp', None, None, 'filter'), may hold values from -6 to 6
- kernel: bfloat16 [3, 3, 1024, 1024], P(None, None, 'filter'), may hold values from -0.0625 to 0.0625
- cotangent: bfloat16 [32, 48, 24, 1024], P('dp', 'filter'), may hold values from -6 to 6
Outputs:
- outputs: bfloat16 [32, 48, 24, 1024], P('dp', 'filter')
- input_grad: bfloat16 [32, 48, 24, 1024], P('dp', None, None, 'filter')
- kernel_grad: float32 [1024, 3, 3, 1024], P('dp', None, None, 'filter')
All inputs are finite; a program needn't handle non-finite values.
Results may differ from a plain program's by a relative error of at most 0.001.
Values may be sent and summed in bfloat16 or wider, within the bound.
No kernel may reach another device: no remote copies, remote signals or barrier semaphores. Data moves between devices by JAX's collectives and lax.ppermute only.
A program may use at most 128 MiB of HBM per device.

v0:
```python
import functools

import jax
import jax.numpy as jnp
from jax import lax
from jax.experimental import pallas as pl
from jax.experimental.pallas import tpu as pltpu
from jax.sharding import Mesh, PartitionSpec as P

F32 = jnp.float32
BF16 = jnp.bfloat16
F16 = jnp.float16
STEPS = (64, 32, 16, 8, 4, 2, 1)


def build_patches(width, x_ref, pad_ref, patch_ref):
    cells, chans = x_ref.shape
    value = x_ref[...].astype(F32)
    column = lax.rem(lax.broadcasted_iota(jnp.int32, value.shape, 0), width)
    left = jnp.where(column == 0, 0.0, pltpu.roll(value, 1, 0))
    right = jnp.where(column == width - 1, 0.0, pltpu.roll(value, cells - 1, 0))
    for b, shifted in enumerate((left, value, right)):
        pad_ref[b, :width, :] = jnp.zeros((width, chans), BF16)
        pad_ref[b, width : width + cells, :] = shifted.astype(BF16)
        pad_ref[b, width + cells :, :] = jnp.zeros((width, chans), BF16)
    for a in range(3):
        for b in range(3):
            tap = 3 * a + b
            patch_ref[:, tap * chans : (tap + 1) * chans] = pad_ref[
                b, a * width : a * width + cells, :
            ]


def forward_kernel(width, x_ref, kernel_ref, out_ref, pad_ref, patch_ref):
    @pl.when(pl.program_id(0) == 0)
    def _():
        build_patches(width, x_ref, pad_ref, patch_ref)

    out_ref[...] = jnp.dot(patch_ref[...], kernel_ref[...], preferred_element_type=F32)


def forward_partial(width, x, weights):
    cells, chans = x.shape
    taps, channels = weights.shape
    block = channels // 4
    x = pltpu.with_memory_space_constraint(x, pltpu.HBM)
    weights = pltpu.with_memory_space_constraint(weights, pltpu.HBM)
    return pl.pallas_call(
        functools.partial(forward_kernel, width),
        out_shape=pltpu.HBM((cells, channels), F32),
        grid=(4,),
        in_specs=[
            pl.BlockSpec((cells, chans), lambda i: (0, 0)),
            pl.BlockSpec((taps, block), lambda i: (0, i)),
        ],
        out_specs=pl.BlockSpec((cells, block), lambda i: (0, i)),
        scratch_shapes=[
            pltpu.VMEM((3, cells + 2 * width, chans), BF16),
            pltpu.VMEM((cells, taps), BF16),
        ],
        compiler_params=pltpu.CompilerParams(vmem_limit_bytes=16 << 20),
        name="forward",
    )(x, weights)


def exponent(top):
    power = jnp.ones_like(top)
    count = jnp.zeros_like(top)
    for step in STEPS:
        fits = top * (2.0**step) < 32768.0
        factor = jnp.where(fits, 2.0**step, 1.0)
        top = top * factor
        power = power * factor
        count = count + jnp.where(fits, float(step), 0.0)
    return power, count


def inverse(count):
    power = jnp.ones_like(count)
    for step in STEPS:
        has = count >= step
        power = power * jnp.where(has, 2.0**-step, 1.0)
        count = count - jnp.where(has, float(step), 0.0)
    return power


def split_kernel(cores, share, core_ref, cot_ref, out_ref):
    rows, channels = cot_ref.shape
    half = channels // cores
    source = lax.broadcasted_iota(jnp.int32, (channels, half), 0)
    target = lax.broadcasted_iota(jnp.int32, (channels, half), 1)
    place = (target // share) * (cores * share) + lax.rem(target, share)
    core = core_ref[0]
    top = jnp.max(jnp.abs(cot_ref[...].astype(F32)), axis=0, keepdims=True)
    top = jnp.max(top, axis=1, keepdims=True)
    power, count = exponent(jnp.broadcast_to(top, (8, half)))
    for slot, owner in ((0, 1 - core), (1, core)):
        pick = jnp.where(source == place + owner * share, 1.0, 0.0).astype(BF16)
        value = jnp.dot(cot_ref[...], pick, preferred_element_type=F32)
        out_ref[slot, :rows, :] = value * power[:1]
        out_ref[slot, rows:, :] = count


def split_by_core(core, cot, share):
    rows, channels = cot.shape
    return pl.pallas_call(
        functools.partial(split_kernel, 2, share),
        out_shape=jax.ShapeDtypeStruct((2, rows + 8, channels // 2), F32),
        in_specs=[
            pl.BlockSpec(memory_space=pltpu.SMEM),
            pl.BlockSpec(memory_space=pltpu.VMEM),
        ],
        out_specs=pl.BlockSpec(memory_space=pltpu.VMEM),
        compiler_params=pltpu.CompilerParams(vmem_limit_bytes=16 << 20),
        name="split_by_core",
    )(core, cot)


def multiply_turned(scale, cot_ref, patch_ref, grad_ref, turned_ref):
    turned = cot_ref[...].T
    turned_ref[...] = turned
    grad = scale * jnp.dot(turned, patch_ref[...], preferred_element_type=F32)
    chips, taps, share, chans = grad_ref.shape
    for chip in range(chips):
        for tap in range(taps):
            grad_ref[chip, tap] = grad[
                chip * share : (chip + 1) * share, tap * chans : (tap + 1) * chans
            ]


def first_kernel(width, scale, x_ref, all_ref, *refs):
    grad_ref, turned_ref, mine_ref, patch_ref, pad_ref, cot_ref = refs
    build_patches(width, x_ref, pad_ref, patch_ref)
    groups, _, rows, _ = all_ref.shape
    rows = rows - 8
    for slot, ref in ((0, cot_ref), (1, mine_ref)):
        for group in range(groups):
            power = inverse(all_ref[group, slot, rows:, :].astype(F32))
            value = all_ref[group, slot, :rows, :].astype(F32) * power[:1]
            ref[group * rows : (group + 1) * rows, :] = value.astype(BF16)
    multiply_turned(scale, cot_ref, patch_ref, grad_ref, turned_ref)


def weight_first(width, scale, share, x, gathered):
    cells, chans = x.shape
    half = gathered.shape[3]
    vmem = pl.BlockSpec(memory_space=pltpu.VMEM)
    return pl.pallas_call(
        functools.partial(first_kernel, width, scale),
        out_shape=(
            jax.ShapeDtypeStruct((half // share, 9, share, chans), F32),
            jax.ShapeDtypeStruct((half, cells), BF16),
            jax.ShapeDtypeStruct((cells, half), BF16),
            jax.ShapeDtypeStruct((cells, 9 * chans), BF16),
        ),
        in_specs=[vmem, vmem],
        out_specs=(vmem,) * 4,
        scratch_shapes=[
            pltpu.VMEM((3, cells + 2 * width, chans), BF16),
            pltpu.VMEM((cells, half), BF16),
        ],
        compiler_params=pltpu.CompilerParams(vmem_limit_bytes=24 << 20),
        name="weight_first",
    )(x, gathered)


def second_kernel(scale, cot_ref, patch_ref, grad_ref, turned_ref):
    multiply_turned(scale, cot_ref, patch_ref, grad_ref, turned_ref)


def weight_second(scale, share, cot, patches):
    cells, half = cot.shape
    chans = patches.shape[1] // 9
    vmem = pl.BlockSpec(memory_space=pltpu.VMEM)
    return pl.pallas_call(
        functools.partial(second_kernel, scale),
        out_shape=(
            jax.ShapeDtypeStruct((half // share, 9, share, chans), F32),
            jax.ShapeDtypeStruct((half, cells), BF16),
        ),
        in_specs=[vmem, vmem],
        out_specs=(vmem, vmem),
        compiler_params=pltpu.CompilerParams(vmem_limit_bytes=24 << 20),
        name="weight_second",
    )(cot, patches)


def input_kernel(width, share, core_ref, theirs_ref, mine_ref, kernel_ref, out_ref, cot_ref):
    cells, chans = out_ref.shape
    chips = theirs_ref.shape[0] // share
    core = core_ref[0]
    for ref, owner in ((theirs_ref, 1 - core), (mine_ref, core)):
        for chip in range(chips):
            start = pl.multiple_of((2 * chip + owner) * share, share)
            cot_ref[pl.ds(start, share), :] = ref[chip * share : (chip + 1) * share, :]
    spread = jnp.dot(kernel_ref[...], cot_ref[...], preferred_element_type=F32)
    cell = lax.broadcasted_iota(jnp.int32, (chans, cells), 1)
    column = lax.rem(cell, width)
    total = None
    for b in range(3):
        part = None
        for a in range(3):
            tap = 3 * a + b
            term = spread[tap * chans : (tap + 1) * chans, :]
            if a == 0:
                term = jnp.where(cell < cells - width, pltpu.roll(term, cells - width, 1), 0.0)
            if a == 2:
                term = jnp.where(cell >= width, pltpu.roll(term, width, 1), 0.0)
            part = term if part is None else part + term
        if b == 0:
            part = jnp.where(column < width - 1, pltpu.roll(part, cells - 1, 1), 0.0)
        if b == 2:
            part = jnp.where(column > 0, pltpu.roll(part, 1, 1), 0.0)
        total = part if total is None else total + part
    out_ref[...] = total.T.astype(BF16)


def input_gradient(width, share, core, theirs, mine, weights):
    cells = theirs.shape[1]
    chans = weights.shape[0] // 9
    vmem = pl.BlockSpec(memory_space=pltpu.VMEM)
    return pl.pallas_call(
        functools.partial(input_kernel, width, share),
        out_shape=jax.ShapeDtypeStruct((cells, chans), BF16),
        in_specs=[pl.BlockSpec(memory_space=pltpu.SMEM)] + [vmem] * 3,
        out_specs=vmem,
        scratch_shapes=[pltpu.VMEM((weights.shape[1], cells), BF16)],
        compiler_params=pltpu.CompilerParams(vmem_limit_bytes=24 << 20),
        name="input_grad",
    )(core, theirs, mine, weights)


def shrink(value):
    taps = value.shape[1]
    power, count = exponent(jnp.max(jnp.abs(value), axis=(1, 3), keepdims=True))
    wide = jnp.pad(value, ((0, 0), (0, 1), (0, 0), (0, 0)))
    tap = lax.broadcasted_iota(jnp.int32, wide.shape, 1)
    return jnp.where(tap < taps, wide * power, count).astype(F16)


def grow(packed):
    taps = packed.shape[1] - 1
    power = inverse(packed[:, taps:, :, :1].astype(F32))
    return packed[:, :taps].astype(F32) * power


def on_device(inputs, kernel, cotangent):
    height, width, local_in = inputs.shape[1:]
    channels = kernel.shape[3]
    groups = lax.axis_size("filter")
    chips = lax.axis_size("chip")
    samples = chips * lax.axis_size("core")
    share = channels // samples
    cells = height * width
    x = inputs.reshape(cells, local_in)
    weights = kernel.reshape(9 * local_in, channels)
    rows = cells // groups
    cot = cotangent.reshape(rows, channels)
    core = lax.axis_index("core").astype(jnp.int32).reshape(1)
    scale = 1.0 / float(samples * cells) ** 0.5

    both = split_by_core(core, cot, share)
    partial = forward_partial(width, x, weights)
    summed = lax.psum_scatter(partial, "filter", scatter_dimension=0, tiled=True)
    outputs = summed.astype(BF16).reshape(cotangent.shape)
    gathered = lax.all_gather(both.astype(F16), "filter", axis=0).astype(BF16)
    theirs_grad, theirs_turned, mine_whole, patches = weight_first(
        width, scale, share, x, gathered
    )
    received = lax.ppermute(theirs_grad, "core", [(0, 1), (1, 0)])
    mine_grad, mine_turned = weight_second(scale, share, mine_whole, patches)
    packed = shrink(mine_grad + received)
    input_grad = input_gradient(width, share, core, theirs_turned, mine_turned, weights)
    input_grad = input_grad.reshape(inputs.shape)

    packed = lax.all_to_all(packed, "chip", 0, 0, tiled=True)
    kernel_grad = jnp.sum(grow(packed), axis=0).transpose(1, 0, 2)
    return (outputs, input_grad, kernel_grad.reshape(share, 3, 3, local_in))


def solution(mesh):
    samples, groups = mesh.devices.shape
    split = Mesh(
        mesh.devices.reshape(samples // 2, 2, groups), ("chip", "core", "filter")
    )
    dp = ("chip", "core")
    return jax.shard_map(
        on_device,
        mesh=split,
        in_specs=(
            P(dp, None, None, "filter"),
            P(None, None, "filter", None),
            P(dp, "filter", None, None),
        ),
        out_specs=(
            P(dp, "filter", None, None),
            P(dp, None, None, "filter"),
            P(dp, None, None, "filter"),
        ),
        check_vma=False,
    )
```

profile of v0, /device:TPU:1, one launch (start us, length us, event | category | flops | bytes accessed | tf_op | source)
XLA Modules:
  0.0 117.1 jit_solution(13716273110845142240)
XLA Ops:
  7.2 0.0 reduce-scatter.2.cloned.1.call-start
  7.2 7.6 %forward.1 = f32[1152,1024]{1,0:T(8,128)} custom-call(bf16[1152,128]{1,0:T(8,128)(2,1)} %bitcast.13, bf16[1152,1024]{1,0:T(8,128)(2,1)} %bitcast.11), custom_call_target="tpu_custom_call" | custom-call | tf_op jit(solution)/shard_map/forward/pallas_call | solution.py:48
  14.8 0.0 reduce-scatter.2.cloned.1.call-update
  14.8 0.9 copy-done.4
  15.7 0.6 split_by_core.1
  16.5 45.9 %all-gather.2 = f16[16,152,512]{2,1,0:T(8,128)(2,1)S(1)} all-gather(f16[2,152,512]{2,1,0:T(8,128)(2,1)S(1)} %convert_element_type.21), channel_id=2, replica_groups=mesh['chip'=16,'core'=2,'filter'=8] {'filter'}, dimensions={0}, use_global_device_ids=true | all-gather | bytes 2801664 | tf_op jit(solution)/shard_map/all_gather | solution.py:266
  62.4 0.5 convert_element_type.26
  62.9 0.5 copy-done.1
  63.3 3.0 %weight_first.1 = (f32[16,9,32,128]{3,2,1,0:T(8,128)S(1)}, bf16[512,1152]{1,0:T(8,128)(2,1)S(1)}, bf16[1152,512]{1,0:T(8,128)(2,1)S(1)}, bf16[1152,1152]{1,0:T(8,128)(2,1)S(1)}) custom-call(bf16[1152,128]{1,0:T(8,128)(2,1)S(1)} %bitcast.14, bf16[8,2,152,512]{3,2,1,0:T(8,128)(2,1)S(1)} %bitcast.10), custom_call_target="tpu_custom_call" | custom-call | tf_op jit(solution)/shard_map/weight_first/pallas_call | solution.py:148
  66.4 5.2 %collective-permute-start = (f32[16,9,32,128]{3,2,1,0:T(8,128)S(1)}, f32[16,9,32,128]{3,2,1,0:T(8,128)S(1)}, u32[]{:S(2)}, u32[]{:S(2)}) collective-permute-start(f32[16,9,32,128]{3,2,1,0:T(8,128)S(1)} %get-tuple-element.14), channel_id=1, source_target_pairs={{0,8},{8,0},{1,9},{9,1},{2,10},{10,2},{3,11},{11,3},{4,12},{12,4},... | collective-permute-start | bytes 7077896 | tf_op jit(solution)/shard_map/ppermute | solution.py:270
  71.6 1.9 %weight_second.1 = (f32[16,9,32,128]{3,2,1,0:T(8,128)S(1)}, bf16[512,1152]{1,0:T(8,128)(2,1)S(1)}) custom-call(bf16[1152,512]{1,0:T(8,128)(2,1)S(1)} %get-tuple-element.10.cot_ref, bf16[1152,1152]{1,0:T(8,128)(2,1)S(1)} %get-tuple-element.11.patch_ref), custom_call_target="tpu_custom_call" | custom-call | tf_op jit(solution)/shard_map/weight_second/pallas_call | solution.py:175
  73.4 0.0 copy-start.2
  73.4 2.3 %collective-permute-done = f32[16,9,32,128]{3,2,1,0:T(8,128)S(1)} collective-permute-done((f32[16,9,32,128]{3,2,1,0:T(8,128)S(1)}, f32[16,9,32,128]{3,2,1,0:T(8,128)S(1)}, u32[]{:S(2)}, u32[]{:S(2)}) %collective-permute-start) | collective-permute-done | bytes 2359328 | tf_op jit(solution)/shard_map/ppermute | solution.py:270
  75.7 0.4 abs_reduce_fusion
  76.2 0.0 copy-done.2
  76.2 0.0 copy-start
  76.2 1.6 %select_convert_fusion = f16[16,10,32,128]{3,2,1,0:T(8,128)(2,1)} fusion(f32[16,9,32,128]{3,2,1,0:T(8,128)S(1)} %get-tuple-element.16, f32[16,32]{1,0:T(8,128)S(1)} %get-tuple-element.18, f32[16,32]{1,0:T(8,128)S(1)} %get-tuple-element.17, pred[10]{0:T(512)(128)(4,1)S(1)} %iota_compare_fusion), kind=kLoop, calls=%fused_computation | loop fusion | flops 1966080 | bytes 3674122 | tf_op jit(solution)/shard_map/convert_element_type | solution.py:238
  77.8 6.9 %all-to-all-start = ((f16[16,10,32,128]{3,2,1,0:T(8,128)(2,1)}), f16[16,10,32,128]{3,2,1,0:T(8,128)(2,1)}, u32[]{:S(2)}, u32[]{:S(2)}) async-start(f16[16,10,32,128]{3,2,1,0:T(8,128)(2,1)} %select_convert_fusion), calls=%async_computation.1 | async-start | bytes 2621440 | tf_op jit(solution)/shard_map/all_to_all | solution.py:276
  84.7 1.3 %copy-done.3 = bf16[512,1152]{1,0:T(8,128)(2,1)S(1)} copy-done((bf16[512,1152]{1,0:T(8,128)(2,1)S(1)}, bf16[512,1152]{1,0:T(8,128)(2,1)}, u32[]{:S(2)}) %copy-start.3) | copy-done | bytes 1179672
  86.0 4.6 %input_grad.1 = bf16[1152,128]{1,0:T(8,128)(2,1)} custom-call(s32[1]{0:T(128)} %bitcast.3.core_ref, bf16[512,1152]{1,0:T(8,128)(2,1)S(1)} %get-tuple-element.9.theirs_ref, bf16[512,1152]{1,0:T(8,128)(2,1)S(1)} %copy-done.3, bf16[1152,1024]{1,0:T(8,128)(2,1)S(1)} %bitcast.12), custom_call_target="tpu_custom_call" | custom-call | tf_op jit(solution)/shard_map/input_grad/pallas_call | solution.py:222
  90.6 14.3 %all-to-all-done = f16[16,10,32,128]{3,2,1,0:T(8,128)(2,1)} async-done(((f16[16,10,32,128]{3,2,1,0:T(8,128)(2,1)}), f16[16,10,32,128]{3,2,1,0:T(8,128)(2,1)}, u32[]{:S(2)}, u32[]{:S(2)}) %all-to-all-start) | async-done | bytes 1310752 | tf_op jit(solution)/shard_map/all_to_all | solution.py:276
  104.9 1.3 %multiply_reduce_fusion.1 = f32[16,32]{1,0:T(8,128)S(1)} fusion(f16[16,10,32,128]{3,2,1,0:T(8,128)(2,1)} %all-to-all-done), kind=kLoop, calls=%fused_computation.5 | loop fusion | flops 16896 | bytes 3072 | tf_op jit(solution)/shard_map/mul | solution.py:82
  106.2 2.3 %multiply_reduce_fusion = f32[9,32,128]{2,1,0:T(8,128)} fusion(f16[16,10,32,128]{3,2,1,0:T(8,128)(2,1)} %all-to-all-done, f32[16,32]{1,0:T(8,128)S(1)} %multiply_reduce_fusion.1), kind=kLoop, calls=%fused_computation.1 | loop fusion | flops 1732608 | bytes 1329152 | tf_op jit(solution)/shard_map/reduce_sum | solution.py:277
  108.5 1.8 %convert_element_type.20 = bf16[144,1024]{1,0:T(8,128)(2,1)} convert(f32[144,1024]{1,0:T(8,128)} %reduce-scatter.2.cloned.1.call-done) | non-fusion elementwise | flops 147456 | bytes 884736 | tf_op jit(solution)/shard_map/convert_element_type | solution.py:265
  (8 shorter events, 0.1 us)
Async XLA Ops:
  7.2 101.3 %reduce-scatter.2.cloned.1.call-start = ((), (), s32[]{:S(2)}) async-start(), calls=%async_computation.2 | async-start | bytes 5308416 | tf_op jit(solution)/shard_map/reduce_scatter | solution.py:264
  14.8 1.0 copy-start.4
  62.4 1.0 copy-start.1
  66.4 9.4 %collective-permute-start = (f32[16,9,32,128]{3,2,1,0:T(8,128)S(1)}, f32[16,9,32,128]{3,2,1,0:T(8,128)S(1)}, u32[]{:S(2)}, u32[]{:S(2)}) collective-permute-start(f32[16,9,32,128]{3,2,1,0:T(8,128)S(1)} %get-tuple-element.14), channel_id=1, source_target_pairs={{0,8},{8,0},{1,9},{9,1},{2,10},{10,2},{3,11},{11,3},{4,12},{12,4},... | collective-permute-start | bytes 7077896 | tf_op jit(solution)/shard_map/ppermute | solution.py:270
  73.4 2.7 %copy-start.2 = (bf16[512,1152]{1,0:T(8,128)(2,1)}, bf16[512,1152]{1,0:T(8,128)(2,1)S(1)}, u32[]{:S(2)}) copy-start(bf16[512,1152]{1,0:T(8,128)(2,1)S(1)} %get-tuple-element.12.mine_ref) | copy-start | bytes 3538948
  76.2 8.5 %copy-start = (bf16[3,3,128,1024]{3,2,1,0:T(8,128)(2,1)S(1)}, bf16[3,3,128,1024]{3,2,1,0:T(8,128)(2,1)}, u32[]{:S(2)}) copy-start(bf16[3,3,128,1024]{3,2,1,0:T(8,128)(2,1)} %param.4) | copy-start | bytes 7077892
  77.8 27.1 %all-to-all-start = ((f16[16,10,32,128]{3,2,1,0:T(8,128)(2,1)}), f16[16,10,32,128]{3,2,1,0:T(8,128)(2,1)}, u32[]{:S(2)}, u32[]{:S(2)}) async-start(f16[16,10,32,128]{3,2,1,0:T(8,128)(2,1)} %select_convert_fusion), calls=%async_computation.1 | async-start | bytes 2621440 | tf_op jit(solution)/shard_map/all_to_all | solution.py:276
  84.7 1.3 %copy-start.3 = (bf16[512,1152]{1,0:T(8,128)(2,1)S(1)}, bf16[512,1152]{1,0:T(8,128)(2,1)}, u32[]{:S(2)}) copy-start(bf16[512,1152]{1,0:T(8,128)(2,1)} %copy-done.2) | copy-start | bytes 3538948
Sparse Core Ops, SparseCore 0:
  14.9 79.9 reduce-scatter.1
where the time goes:
time: 118 us; the launch traced here: 117 us
  blocking collectives  45.9 us (39%)
  Pallas kernels  17.7 us (15%)
  waiting for transfers between devices  16.6 us (14%)
  between operations  14.1 us (12%)
  starting transfers between devices  12.1 us (10%)
  other arithmetic  7.98 us (7%)
  local copies, waits for them, and re-layouts  2.71 us (2%)
    all_gather x1, blocking collectives, on_device(): gathered = lax.all_gather(both.astype(F16), 'filter', axis=0).astype(BF16)  45.9 us
    all_to_all x1, waiting for transfers between devices, on_device(): packed = lax.all_to_all(packed, 'chip', 0, 0, tiled=True)  14.3 us
    pallas_call x1, Pallas kernels, forward_partial(): pl.pallas_call(functools.partial(forward_kernel, width), out_shape=pltpu....  7.57 us
    all_to_all x1, starting transfers between devices, on_device(): packed = lax.all_to_all(packed, 'chip', 0, 0, tiled=True)  6.89 us
    ppermute x1, starting transfers between devices, on_device(): received = lax.ppermute(theirs_grad, 'core', [(0, 1), (1, 0)])  5.19 us
    pallas_call x1, Pallas kernels, input_gradient(): pl.pallas_call(functools.partial(input_kernel, width, share), out_shape=j...  4.57 us
    pallas_call x1, Pallas kernels, weight_first(): pl.pallas_call(functools.partial(first_kernel, width, scale), out_shape=(...  3.01 us
    unnamed x10, local copies, waits for them, and re-layouts  2.71 us
  transfers between devices with their start and end apart: 3, of which 2 were waited for; matrix products, arithmetic and copies ran while one was open for 5% of the time, Pallas kernels for 9%

commit v1 on v0

--- a/solution.py
+++ b/solution.py
@@ -31,38 +31,6 @@
             ]
 
 
-def forward_kernel(width, x_ref, kernel_ref, out_ref, pad_ref, patch_ref):
-    @pl.when(pl.program_id(0) == 0)
-    def _():
-        build_patches(width, x_ref, pad_ref, patch_ref)
-
-    out_ref[...] = jnp.dot(patch_ref[...], kernel_ref[...], preferred_element_type=F32)
-
-
-def forward_partial(width, x, weights):
-    cells, chans = x.shape
-    taps, channels = weights.shape
-    block = channels // 4
-    x = pltpu.with_memory_space_constraint(x, pltpu.HBM)
-    weights = pltpu.with_memory_space_constraint(weights, pltpu.HBM)
-    return pl.pallas_call(
-        functools.partial(forward_kernel, width),
-        out_shape=pltpu.HBM((cells, channels), F32),
-        grid=(4,),
-        in_specs=[
-            pl.BlockSpec((cells, chans), lambda i: (0, 0)),
-            pl.BlockSpec((taps, block), lambda i: (0, i)),
-        ],
-        out_specs=pl.BlockSpec((cells, block), lambda i: (0, i)),
-        scratch_shapes=[
-            pltpu.VMEM((3, cells + 2 * width, chans), BF16),
-            pltpu.VMEM((cells, taps), BF16),
-        ],
-        compiler_params=pltpu.CompilerParams(vmem_limit_bytes=16 << 20),
-        name="forward",
-    )(x, weights)
-
-
 def exponent(top):
     power = jnp.ones_like(top)
     count = jnp.zeros_like(top)
@@ -84,84 +52,108 @@
     return power
 
 
-def split_kernel(cores, share, core_ref, cot_ref, out_ref):
+def split_by_core(share, core, cot_ref, out_ref):
     rows, channels = cot_ref.shape
-    half = channels // cores
+    half = channels // 2
     source = lax.broadcasted_iota(jnp.int32, (channels, half), 0)
     target = lax.broadcasted_iota(jnp.int32, (channels, half), 1)
-    place = (target // share) * (cores * share) + lax.rem(target, share)
-    core = core_ref[0]
+    place = (target // share) * (2 * share) + lax.rem(target, share)
     top = jnp.max(jnp.abs(cot_ref[...].astype(F32)), axis=0, keepdims=True)
     top = jnp.max(top, axis=1, keepdims=True)
     power, count = exponent(jnp.broadcast_to(top, (8, half)))
     for slot, owner in ((0, 1 - core), (1, core)):
         pick = jnp.where(source == place + owner * share, 1.0, 0.0).astype(BF16)
         value = jnp.dot(cot_ref[...], pick, preferred_element_type=F32)
-        out_ref[slot, :rows, :] = value * power[:1]
-        out_ref[slot, rows:, :] = count
-
-
-def split_by_core(core, cot, share):
-    rows, channels = cot.shape
-    return pl.pallas_call(
-        functools.partial(split_kernel, 2, share),
-        out_shape=jax.ShapeDtypeStruct((2, rows + 8, channels // 2), F32),
+        out_ref[slot * rows : (slot + 1) * rows, :] = value * power[:1]
+    out_ref[2 * rows :, :] = count
+
+
+def forward_kernel(width, share, core_ref, x_ref, cot_ref, kernel_ref, *refs):
+    out_ref, both_ref, patch_ref, pad_ref = refs
+
+    @pl.when(pl.program_id(0) == 0)
+    def _():
+        build_patches(width, x_ref, pad_ref, patch_ref)
+        split_by_core(share, core_ref[0], cot_ref, both_ref)
+
+    out_ref[...] = jnp.dot(patch_ref[...], kernel_ref[...], preferred_element_type=F32)
+
+
+def forward_partial(width, share, core, x, cot, weights):
+    cells, chans = x.shape
+    taps, channels = weights.shape
+    rows = 2 * cot.shape[0] + 8
+    block = channels // 4
+    x = pltpu.with_memory_space_constraint(x, pltpu.HBM)
+    cot = pltpu.with_memory_space_constraint(cot, pltpu.HBM)
+    weights = pltpu.with_memory_space_constraint(weights, pltpu.HBM)
+    return pl.pallas_call(
+        functools.partial(forward_kernel, width, share),
+        out_shape=(
+            pltpu.HBM((cells, channels), F32),
+            jax.ShapeDtypeStruct((rows, channels // 2), F32),
+            jax.ShapeDtypeStruct((cells, taps), BF16),
+        ),
+        grid=(4,),
         in_specs=[
             pl.BlockSpec(memory_space=pltpu.SMEM),
-            pl.BlockSpec(memory_space=pltpu.VMEM),
+            pl.BlockSpec((cells, chans), lambda i: (0, 0)),
+            pl.BlockSpec(cot.shape, lambda i: (0, 0)),
+            pl.BlockSpec((taps, block), lambda i: (0, i)),
         ],
-        out_specs=pl.BlockSpec(memory_space=pltpu.VMEM),
-        compiler_params=pltpu.CompilerParams(vmem_limit_bytes=16 << 20),
-        name="split_by_core",
-    )(core, cot)
+        out_specs=(
+            pl.BlockSpec((cells, block), lambda i: (0, i)),
+            pl.BlockSpec((rows, channels // 2), lambda i: (0, 0)),
+            pl.BlockSpec((cells, taps), lambda i: (0, 0)),
+        ),
+        scratch_shapes=[pltpu.VMEM((3, cells + 2 * width, chans), BF16)],
+        compiler_params=pltpu.CompilerParams(vmem_limit_bytes=24 << 20),
+        name="forward",
+    )(core, x, cot, weights)
 
 
 def multiply_turned(scale, cot_ref, patch_ref, grad_ref, turned_ref):
     turned = cot_ref[...].T
     turned_ref[...] = turned
     grad = scale * jnp.dot(turned, patch_ref[...], preferred_element_type=F32)
-    chips, taps, share, chans = grad_ref.shape
+    chips, rows, chans = grad_ref.shape
+    share = rows // 9
     for chip in range(chips):
-        for tap in range(taps):
-            grad_ref[chip, tap] = grad[
+        for tap in range(9):
+            grad_ref[chip, tap * share : (tap + 1) * share, :] = grad[
                 chip * share : (chip + 1) * share, tap * chans : (tap + 1) * chans
             ]
 
 
-def first_kernel(width, scale, x_ref, all_ref, *refs):
-    grad_ref, turned_ref, mine_ref, patch_ref, pad_ref, cot_ref = refs
-    build_patches(width, x_ref, pad_ref, patch_ref)
-    groups, _, rows, _ = all_ref.shape
-    rows = rows - 8
-    for slot, ref in ((0, cot_ref), (1, mine_ref)):
-        for group in range(groups):
-            power = inverse(all_ref[group, slot, rows:, :].astype(F32))
-            value = all_ref[group, slot, :rows, :].astype(F32) * power[:1]
+def first_kernel(scale, patch_ref, all_ref, grad_ref, turned_ref, mine_ref, cot_ref):
+    groups = all_ref.shape[0]
+    rows = (all_ref.shape[1] - 8) // 2
+    for group in range(groups):
+        power = inverse(all_ref[group, 2 * rows :, :].astype(F32))[:1]
+        for slot, ref in ((0, cot_ref), (1, mine_ref)):
+            value = all_ref[group, slot * rows : (slot + 1) * rows, :].astype(F32) * power
             ref[group * rows : (group + 1) * rows, :] = value.astype(BF16)
     multiply_turned(scale, cot_ref, patch_ref, grad_ref, turned_ref)
 
 
-def weight_first(width, scale, share, x, gathered):
-    cells, chans = x.shape
-    half = gathered.shape[3]
+def weight_first(scale, share, patches, gathered):
+    cells = patches.shape[0]
+    chans = patches.shape[1] // 9
+    half = gathered.shape[2]
     vmem = pl.BlockSpec(memory_space=pltpu.VMEM)
     return pl.pallas_call(
-        functools.partial(first_kernel, width, scale),
+        functools.partial(first_kernel, scale),
         out_shape=(
-            jax.ShapeDtypeStruct((half // share, 9, share, chans), F32),
+            jax.ShapeDtypeStruct((half // share, 9 * share, chans), F32),
             jax.ShapeDtypeStruct((half, cells), BF16),
             jax.ShapeDtypeStruct((cells, half), BF16),
-            jax.ShapeDtypeStruct((cells, 9 * chans), BF16),
         ),
         in_specs=[vmem, vmem],
-        out_specs=(vmem,) * 4,
-        scratch_shapes=[
-            pltpu.VMEM((3, cells + 2 * width, chans), BF16),
-            pltpu.VMEM((cells, half), BF16),
-        ],
+        out_specs=(vmem,) * 3,
+        scratch_shapes=[pltpu.VMEM((cells, half), BF16)],
         compiler_params=pltpu.CompilerParams(vmem_limit_bytes=24 << 20),
         name="weight_first",
-    )(x, gathered)
+    )(patches, gathered)
 
 
 def second_kernel(scale, cot_ref, patch_ref, grad_ref, turned_ref):
@@ -175,7 +167,7 @@
     return pl.pallas_call(
         functools.partial(second_kernel, scale),
         out_shape=(
-            jax.ShapeDtypeStruct((half // share, 9, share, chans), F32),
+            jax.ShapeDtypeStruct((half // share, 9 * share, chans), F32),
             jax.ShapeDtypeStruct((half, cells), BF16),
         ),
         in_specs=[vmem, vmem],
@@ -231,17 +223,16 @@
 
 
 def shrink(value):
-    taps = value.shape[1]
-    power, count = exponent(jnp.max(jnp.abs(value), axis=(1, 3), keepdims=True))
-    wide = jnp.pad(value, ((0, 0), (0, 1), (0, 0), (0, 0)))
-    tap = lax.broadcasted_iota(jnp.int32, wide.shape, 1)
-    return jnp.where(tap < taps, wide * power, count).astype(F16)
+    rows = value.shape[1]
+    power, count = exponent(jnp.max(jnp.abs(value), axis=(1, 2), keepdims=True))
+    wide = jnp.pad(value, ((0, 0), (0, 8), (0, 0)))
+    row = lax.broadcasted_iota(jnp.int32, wide.shape, 1)
+    return jnp.where(row < rows, wide * power, count).astype(F16)
 
 
 def grow(packed):
-    taps = packed.shape[1] - 1
-    power = inverse(packed[:, taps:, :, :1].astype(F32))
-    return packed[:, :taps].astype(F32) * power
+    power = inverse(packed[:, -8:-7, :1].astype(F32))
+    return packed[:, :-8].astype(F32) * power
 
 
 def on_device(inputs, kernel, cotangent):
@@ -259,14 +250,11 @@
     core = lax.axis_index("core").astype(jnp.int32).reshape(1)
     scale = 1.0 / float(samples * cells) ** 0.5
 
-    both = split_by_core(core, cot, share)
-    partial = forward_partial(width, x, weights)
+    partial, both, patches = forward_partial(width, share, core, x, cot, weights)
     summed = lax.psum_scatter(partial, "filter", scatter_dimension=0, tiled=True)
     outputs = summed.astype(BF16).reshape(cotangent.shape)
     gathered = lax.all_gather(both.astype(F16), "filter", axis=0).astype(BF16)
-    theirs_grad, theirs_turned, mine_whole, patches = weight_first(
-        width, scale, share, x, gathered
-    )
+    theirs_grad, theirs_turned, mine_whole = weight_first(scale, share, patches, gathered)
     received = lax.ppermute(theirs_grad, "core", [(0, 1), (1, 0)])
     mine_grad, mine_turned = weight_second(scale, share, mine_whole, patches)
     packed = shrink(mine_grad + received)
@@ -274,7 +262,9 @@
     input_grad = input_grad.reshape(inputs.shape)
 
     packed = lax.all_to_all(packed, "chip", 0, 0, tiled=True)
-    kernel_grad = jnp.sum(grow(packed), axis=0).transpose(1, 0, 2)
+    packed, outputs = lax.optimization_barrier((packed, outputs))
+    kernel_grad = jnp.sum(grow(packed), axis=0).reshape(9, share, local_in)
+    kernel_grad = kernel_grad.transpose(1, 0, 2)
     return (outputs, input_grad, kernel_grad.reshape(share, 3, 3, local_in))
 
 

time: 118 us -> 109 us (0.924)
  waiting for transfers between devices: 16.6 us -> 13.1 us
  blocking collectives: 45.9 us -> 43.5 us
  local copies, waits for them, and re-layouts: 2.71 us -> 1.3 us
  Pallas kernels: 17.7 us -> 16.5 us
    all_to_all x1, waiting for transfers between devices: 14.3 us -> 3.53 us  [on_device(): packed = lax.all_to_all(packed, 'chip', 0, 0, tiled=True)]
    reduce_scatter x1, waiting for transfers between devices: 0.01 us -> 7.31 us  [on_device(): lax.psum_scatter(partial, 'filter', scatter_dimension=0, tiled=True)]
    all_gather x1, blocking collectives: 45.9 us -> 43.5 us  [on_device(): gathered = lax.all_gather(both.astype(F16), 'filter', axis=0).astype(BF16)]
    unnamed x10, local copies, waits for them, and re-layouts: 2.71 us -> 1.3 us
    pallas_call x3 -> x2, Pallas kernels: 11.2 us -> 10.1 us  [the longest x1 7.85 us: forward_partial(): pl.pallas_call(functools.partial(forward_kernel, width, share), out_shape...]
  transfers between devices with their start and end apart: 3 -> 3, of which waited for: 2 -> 3; matrix products, arithmetic and copies ran while one was open for 5% -> 4% of each run, Pallas kernels for 9% -> 8%
where the time goes in v1:
time: 109 us
  blocking collectives  43.5 us (40%)
  Pallas kernels  16.5 us (15%)
  between operations  14.1 us (13%)
  waiting for transfers between devices  13.1 us (12%)
  starting transfers between devices  12.5 us (11%)
  other arithmetic  7.54 us (7%)
  local copies, waits for them, and re-layouts  1.3 us (1%)
    all_gather x1, blocking collectives, on_device(): gathered = lax.all_gather(both.astype(F16), 'filter', axis=0).astype(BF16)  43.5 us
    pallas_call x1, Pallas kernels, forward_partial(): pl.pallas_call(functools.partial(forward_kernel, width, share), out_shape...  7.85 us
    reduce_scatter x1, waiting for transfers between devices, on_device(): lax.psum_scatter(partial, 'filter', scatter_dimension=0, tiled=True)  7.31 us
    all_to_all x1, starting transfers between devices, on_device(): packed = lax.all_to_all(packed, 'chip', 0, 0, tiled=True)  7.14 us
    ppermute x1, starting transfers between devices, on_device(): received = lax.ppermute(theirs_grad, 'core', [(0, 1), (1, 0)])  5.32 us
    pallas_call x1, Pallas kernels, input_gradient(): pl.pallas_call(functools.partial(input_kernel, width, share), out_shape=j...  4.56 us
    all_to_all x1, waiting for transfers between devices, on_device(): packed = lax.all_to_all(packed, 'chip', 0, 0, tiled=True)  3.53 us
    ppermute x1, waiting for transfers between devices, on_device(): received = lax.ppermute(theirs_grad, 'core', [(0, 1), (1, 0)])  2.27 us
  transfers between devices with their start and end apart: 3, of which 3 were waited for; matrix products, arithmetic and copies ran while one was open for 4% of the time, Pallas kernels for 8%

profile of v1, /device:TPU:1, one launch (start us, length us, event | category | flops | bytes accessed | tf_op | source)
XLA Modules:
  0.0 108.6 jit_solution(17172336799131325003)
XLA Ops:
  7.2 0.0 reduce-scatter.2.cloned.1.call-start
  7.2 7.8 %forward.1 = (f32[1152,1024]{1,0:T(8,128)}, f32[296,512]{1,0:T(8,128)S(1)}, bf16[1152,1152]{1,0:T(8,128)(2,1)S(1)}) custom-call(s32[1]{0:T(128)} %bitcast.core_ref, bf16[1152,128]{1,0:T(8,128)(2,1)} %bitcast.15, bf16[144,1024]{1,0:T(8,128)(2,1)} %bitcast.16, bf16[1152,1024]{1,0:T(8,128)(2,1)} %bitcast.13), custom_call_target="tpu_custom_call" | custom-call | tf_op jit(solution)/shard_map/forward/pallas_call | solution.py:90
  15.1 0.0 reduce-scatter.2.cloned.1.call-update
  15.1 43.5 %all-gather.2 = f16[2368,512]{1,0:T(8,128)(2,1)S(1)} all-gather(f16[296,512]{1,0:T(8,128)(2,1)S(1)} %convert_element_type.20), channel_id=2, replica_groups=mesh['chip'=16,'core'=2,'filter'=8] {'filter'}, dimensions={0}, use_global_device_ids=true | all-gather | bytes 2727936 | tf_op jit(solution)/shard_map/all_gather | solution.py:256
  58.7 0.5 convert_element_type.26
  59.1 2.2 %weight_first.1 = (f32[16,288,128]{2,1,0:T(8,128)S(1)}, bf16[512,1152]{1,0:T(8,128)(2,1)S(1)}, bf16[1152,512]{1,0:T(8,128)(2,1)S(1)}) custom-call(bf16[1152,1152]{1,0:T(8,128)(2,1)S(1)} %get-tuple-element.13.patch_ref, bf16[8,296,512]{2,1,0:T(8,128)(2,1)S(1)} %bitcast.12), custom_call_target="tpu_custom_call" | custom-call | tf_op jit(solution)/shard_map/weight_first/pallas_call | solution.py:144
  61.3 0.0 copy-start.1
  61.3 5.3 %collective-permute-start = (f32[16,288,128]{2,1,0:T(8,128)S(1)}, f32[16,288,128]{2,1,0:T(8,128)S(1)}, u32[]{:S(2)}, u32[]{:S(2)}) collective-permute-start(f32[16,288,128]{2,1,0:T(8,128)S(1)} %get-tuple-element.17), channel_id=1, source_target_pairs={{0,8},{8,0},{1,9},{9,1},{2,10},{10,2},{3,11},{11,3},{4,12},{12,4},... | collective-permute-start | bytes 7077896 | tf_op jit(solution)/shard_map/ppermute | solution.py:258
  66.7 1.9 %weight_second.1 = (f32[16,288,128]{2,1,0:T(8,128)S(1)}, bf16[512,1152]{1,0:T(8,128)(2,1)S(1)}) custom-call(bf16[1152,512]{1,0:T(8,128)(2,1)S(1)} %get-tuple-element.15.cot_ref, bf16[1152,1152]{1,0:T(8,128)(2,1)S(1)} %get-tuple-element.13.patch_ref), custom_call_target="tpu_custom_call" | custom-call | tf_op jit(solution)/shard_map/weight_second/pallas_call | solution.py:167
  68.5 0.0 copy-start.3
  68.6 2.3 %collective-permute-done = f32[16,288,128]{2,1,0:T(8,128)S(1)} collective-permute-done((f32[16,288,128]{2,1,0:T(8,128)S(1)}, f32[16,288,128]{2,1,0:T(8,128)S(1)}, u32[]{:S(2)}, u32[]{:S(2)}) %collective-permute-start) | collective-permute-done | bytes 2359328 | tf_op jit(solution)/shard_map/ppermute | solution.py:258
  70.8 0.5 abs_reduce_fusion
  71.3 0.0 copy-done.1
  71.3 0.0 copy-done.3
  71.4 0.0 copy-start
  71.4 1.5 %select_convert_fusion = f16[16,296,128]{2,1,0:T(8,128)(2,1)} fusion(f32[16,288,128]{2,1,0:T(8,128)S(1)} %get-tuple-element.24, f32[16]{0:T(128)S(1)} %get-tuple-element.26, f32[16]{0:T(128)S(1)} %get-tuple-element.25, pred[296]{0:T(512)(128)(4,1)S(1)} %iota_compare_fusion), kind=kLoop, calls=%fused_computation | loop fusion | flops 1818624 | bytes 3572136 | tf_op jit(solution)/shard_map/convert_element_type | solution.py:230
  72.8 7.1 %all-to-all-start = ((f16[16,296,128]{2,1,0:T(8,128)(2,1)}), f16[16,296,128]{2,1,0:T(8,128)(2,1)}, u32[]{:S(2)}, u32[]{:S(2)}) async-start(f16[16,296,128]{2,1,0:T(8,128)(2,1)} %select_convert_fusion), calls=%async_computation | async-start | bytes 2424832 | tf_op jit(solution)/shard_map/all_to_all | solution.py:264
  80.0 1.3 %copy-done.4 = bf16[512,1152]{1,0:T(8,128)(2,1)S(1)} copy-done((bf16[512,1152]{1,0:T(8,128)(2,1)S(1)}, bf16[512,1152]{1,0:T(8,128)(2,1)}, u32[]{:S(2)}) %copy-start.4) | copy-done | bytes 1179672
  81.3 4.6 %input_grad.1 = bf16[1152,128]{1,0:T(8,128)(2,1)} custom-call(s32[1]{0:T(128)} %bitcast.core_ref, bf16[512,1152]{1,0:T(8,128)(2,1)S(1)} %copy-done.2, bf16[512,1152]{1,0:T(8,128)(2,1)S(1)} %copy-done.4, bf16[1152,1024]{1,0:T(8,128)(2,1)S(1)} %bitcast.14), custom_call_target="tpu_custom_call" | custom-call | tf_op jit(solution)/shard_map/input_grad/pallas_call | solution.py:214
  85.9 7.3 %reduce-scatter.2.cloned.1.call-done = f32[144,1024]{1,0:T(8,128)} async-done(((f32[1152,1024]{1,0:T(8,128)}), f32[144,1024]{1,0:T(8,128)}) %reduce-scatter.2.cloned.1.call-update) | async-done | bytes 589840 | tf_op jit(solution)/shard_map/reduce_scatter | solution.py:254
  93.2 1.8 %convert_element_type.23 = bf16[144,1024]{1,0:T(8,128)(2,1)} convert(f32[144,1024]{1,0:T(8,128)} %reduce-scatter.2.cloned.1.call-done) | non-fusion elementwise | flops 147456 | bytes 884736 | tf_op jit(solution)/shard_map/convert_element_type | solution.py:255
  95.0 3.5 %all-to-all-done = f16[16,296,128]{2,1,0:T(8,128)(2,1)} async-done(((f16[16,296,128]{2,1,0:T(8,128)(2,1)}), f16[16,296,128]{2,1,0:T(8,128)(2,1)}, u32[]{:S(2)}, u32[]{:S(2)}) %all-to-all-start) | async-done | bytes 1212448 | tf_op jit(solution)/shard_map/all_to_all | solution.py:264
  98.5 1.0 fusion.12
  99.5 2.3 %multiply_reduce_fusion = f32[288,128]{1,0:T(8,128)} fusion(f32[16]{0:T(128)S(1)} %fusion.12, f16[16,296,128]{2,1,0:T(8,128)(2,1)} %all-to-all-done), kind=kLoop, calls=%fused_computation.1 | loop fusion | flops 1732608 | bytes 1327168 | tf_op jit(solution)/shard_map/reduce_sum | solution.py:266
  (7 shorter events, 0.1 us)
Async XLA Ops:
  7.2 86.0 %reduce-scatter.2.cloned.1.call-start = ((), (), s32[]{:S(2)}) async-start(), calls=%async_computation.2 | async-start | bytes 5308416 | tf_op jit(solution)/shard_map/reduce_scatter | solution.py:254
  61.3 10.0 %copy-start.1 = (bf16[512,1152]{1,0:T(8,128)(2,1)}, bf16[512,1152]{1,0:T(8,128)(2,1)S(1)}, u32[]{:S(2)}) copy-start(bf16[512,1152]{1,0:T(8,128)(2,1)S(1)} %get-tuple-element.20.theirs_ref) | copy-start | bytes 3538948
  61.3 9.5 %collective-permute-start = (f32[16,288,128]{2,1,0:T(8,128)S(1)}, f32[16,288,128]{2,1,0:T(8,128)S(1)}, u32[]{:S(2)}, u32[]{:S(2)}) collective-permute-start(f32[16,288,128]{2,1,0:T(8,128)S(1)} %get-tuple-element.17), channel_id=1, source_target_pairs={{0,8},{8,0},{1,9},{9,1},{2,10},{10,2},{3,11},{11,3},{4,12},{12,4},... | collective-permute-start | bytes 7077896 | tf_op jit(solution)/shard_map/ppermute | solution.py:258
  68.5 2.8 %copy-start.3 = (bf16[512,1152]{1,0:T(8,128)(2,1)}, bf16[512,1152]{1,0:T(8,128)(2,1)S(1)}, u32[]{:S(2)}) copy-start(bf16[512,1152]{1,0:T(8,128)(2,1)S(1)} %get-tuple-element.21.mine_ref) | copy-start | bytes 3538948
  71.4 8.6 %copy-start = (bf16[3,3,128,1024]{3,2,1,0:T(8,128)(2,1)S(1)}, bf16[3,3,128,1024]{3,2,1,0:T(8,128)(2,1)}, u32[]{:S(2)}) copy-start(bf16[3,3,128,1024]{3,2,1,0:T(8,128)(2,1)} %param.4) | copy-start | bytes 7077892
  71.4 8.6 %copy-start.2 = (bf16[512,1152]{1,0:T(8,128)(2,1)S(1)}, bf16[512,1152]{1,0:T(8,128)(2,1)}, u32[]{:S(2)}) copy-start(bf16[512,1152]{1,0:T(8,128)(2,1)} %copy-done.1) | copy-start | bytes 3538948
  72.8 25.7 %all-to-all-start = ((f16[16,296,128]{2,1,0:T(8,128)(2,1)}), f16[16,296,128]{2,1,0:T(8,128)(2,1)}, u32[]{:S(2)}, u32[]{:S(2)}) async-start(f16[16,296,128]{2,1,0:T(8,128)(2,1)} %select_convert_fusion), calls=%async_computation | async-start | bytes 2424832 | tf_op jit(solution)/shard_map/all_to_all | solution.py:264
  80.0 1.3 %copy-start.4 = (bf16[512,1152]{1,0:T(8,128)(2,1)S(1)}, bf16[512,1152]{1,0:T(8,128)(2,1)}, u32[]{:S(2)}) copy-start(bf16[512,1152]{1,0:T(8,128)(2,1)} %copy-done.3) | copy-start | bytes 3538948
Sparse Core Ops, SparseCore 0:
  15.2 77.9 reduce-scatter.1

commit v2 on v1

--- a/solution.py
+++ b/solution.py
@@ -55,16 +55,21 @@
 def split_by_core(share, core, cot_ref, out_ref):
     rows, channels = cot_ref.shape
     half = channels // 2
-    source = lax.broadcasted_iota(jnp.int32, (channels, half), 0)
-    target = lax.broadcasted_iota(jnp.int32, (channels, half), 1)
+    source = lax.broadcasted_iota(jnp.int32, (256, 128), 0)
+    target = lax.broadcasted_iota(jnp.int32, (256, 128), 1)
     place = (target // share) * (2 * share) + lax.rem(target, share)
     top = jnp.max(jnp.abs(cot_ref[...].astype(F32)), axis=0, keepdims=True)
     top = jnp.max(top, axis=1, keepdims=True)
     power, count = exponent(jnp.broadcast_to(top, (8, half)))
     for slot, owner in ((0, 1 - core), (1, core)):
         pick = jnp.where(source == place + owner * share, 1.0, 0.0).astype(BF16)
-        value = jnp.dot(cot_ref[...], pick, preferred_element_type=F32)
-        out_ref[slot * rows : (slot + 1) * rows, :] = value * power[:1]
+        for k in range(half // 128):
+            value = jnp.dot(
+                cot_ref[:, 256 * k : 256 * (k + 1)], pick, preferred_element_type=F32
+            )
+            out_ref[slot * rows : (slot + 1) * rows, 128 * k : 128 * (k + 1)] = (
+                value * power[:1, :128]
+            )
     out_ref[2 * rows :, :] = count
 
 
@@ -112,8 +117,8 @@
     )(core, x, cot, weights)
 
 
-def multiply_turned(scale, cot_ref, patch_ref, grad_ref, turned_ref):
-    turned = cot_ref[...].T
+def multiply_turned(scale, cot, patch_ref, grad_ref, turned_ref):
+    turned = cot.T
     turned_ref[...] = turned
     grad = scale * jnp.dot(turned, patch_ref[...], preferred_element_type=F32)
     chips, rows, chans = grad_ref.shape
@@ -125,7 +130,7 @@
             ]
 
 
-def first_kernel(scale, patch_ref, all_ref, grad_ref, turned_ref, mine_ref, cot_ref):
+def first_kernel(scale, patch_ref, all_ref, grad_ref, turned_ref, cot_ref, mine_ref):
     groups = all_ref.shape[0]
     rows = (all_ref.shape[1] - 8) // 2
     for group in range(groups):
@@ -133,7 +138,8 @@
         for slot, ref in ((0, cot_ref), (1, mine_ref)):
             value = all_ref[group, slot * rows : (slot + 1) * rows, :].astype(F32) * power
             ref[group * rows : (group + 1) * rows, :] = value.astype(BF16)
-    multiply_turned(scale, cot_ref, patch_ref, grad_ref, turned_ref)
+    start = cot_ref[:, : turned_ref.shape[0]]
+    multiply_turned(scale, start, patch_ref, grad_ref, turned_ref)
 
 
 def weight_first(scale, share, patches, gathered):
@@ -144,46 +150,53 @@
     return pl.pallas_call(
         functools.partial(first_kernel, scale),
         out_shape=(
-            jax.ShapeDtypeStruct((half // share, 9 * share, chans), F32),
-            jax.ShapeDtypeStruct((half, cells), BF16),
+            jax.ShapeDtypeStruct((half // 2 // share, 9 * share, chans), F32),
+            pltpu.HBM((half // 2, cells), BF16),
             jax.ShapeDtypeStruct((cells, half), BF16),
+            jax.ShapeDtypeStruct((cells, half), BF16),
         ),
         in_specs=[vmem, vmem],
-        out_specs=(vmem,) * 3,
-        scratch_shapes=[pltpu.VMEM((cells, half), BF16)],
+        out_specs=(vmem,) * 4,
         compiler_params=pltpu.CompilerParams(vmem_limit_bytes=24 << 20),
         name="weight_first",
     )(patches, gathered)
 
 
 def second_kernel(scale, cot_ref, patch_ref, grad_ref, turned_ref):
-    multiply_turned(scale, cot_ref, patch_ref, grad_ref, turned_ref)
-
-
-def weight_second(scale, share, cot, patches):
-    cells, half = cot.shape
+    multiply_turned(scale, cot_ref[...], patch_ref, grad_ref, turned_ref)
+
+
+def weight_second(scale, share, cot, patches, parts, part):
+    cells = cot.shape[0]
+    half = cot.shape[1] // parts
     chans = patches.shape[1] // 9
     vmem = pl.BlockSpec(memory_space=pltpu.VMEM)
     return pl.pallas_call(
         functools.partial(second_kernel, scale),
         out_shape=(
             jax.ShapeDtypeStruct((half // share, 9 * share, chans), F32),
-            jax.ShapeDtypeStruct((half, cells), BF16),
-        ),
-        in_specs=[vmem, vmem],
+            pltpu.HBM((half, cells), BF16),
+        ),
+        grid=(1,),
+        in_specs=[pl.BlockSpec((cells, half), lambda i: (0, part)), vmem],
         out_specs=(vmem, vmem),
         compiler_params=pltpu.CompilerParams(vmem_limit_bytes=24 << 20),
         name="weight_second",
     )(cot, patches)
 
 
-def input_kernel(width, share, core_ref, theirs_ref, mine_ref, kernel_ref, out_ref, cot_ref):
+def input_kernel(width, share, core_ref, *refs):
+    early_ref, late_ref, mine_ref, kernel_ref, out_ref, cot_ref = refs
     cells, chans = out_ref.shape
-    chips = theirs_ref.shape[0] // share
     core = core_ref[0]
-    for ref, owner in ((theirs_ref, 1 - core), (mine_ref, core)):
-        for chip in range(chips):
-            start = pl.multiple_of((2 * chip + owner) * share, share)
+    middle = early_ref.shape[0] // share
+    for ref, owner, first in (
+        (early_ref, 1 - core, 0),
+        (late_ref, 1 - core, middle),
+        (mine_ref, core, 0),
+    ):
+        for chip in range(ref.shape[0] // share):
+            start = pl.multiple_of((2 * (first + chip) + owner) * share, share)
             cot_ref[pl.ds(start, share), :] = ref[chip * share : (chip + 1) * share, :]
     spread = jnp.dot(kernel_ref[...], cot_ref[...], preferred_element_type=F32)
     cell = lax.broadcasted_iota(jnp.int32, (chans, cells), 1)
@@ -207,19 +220,19 @@
     out_ref[...] = total.T.astype(BF16)
 
 
-def input_gradient(width, share, core, theirs, mine, weights):
-    cells = theirs.shape[1]
+def input_gradient(width, share, core, early, late, mine, weights):
+    cells = mine.shape[1]
     chans = weights.shape[0] // 9
     vmem = pl.BlockSpec(memory_space=pltpu.VMEM)
     return pl.pallas_call(
         functools.partial(input_kernel, width, share),
         out_shape=jax.ShapeDtypeStruct((cells, chans), BF16),
-        in_specs=[pl.BlockSpec(memory_space=pltpu.SMEM)] + [vmem] * 3,
+        in_specs=[pl.BlockSpec(memory_space=pltpu.SMEM)] + [vmem] * 4,
         out_specs=vmem,
         scratch_shapes=[pltpu.VMEM((weights.shape[1], cells), BF16)],
         compiler_params=pltpu.CompilerParams(vmem_limit_bytes=24 << 20),
         name="input_grad",
-    )(core, theirs, mine, weights)
+    )(core, early, late, mine, weights)
 
 
 def shrink(value):
@@ -231,7 +244,7 @@
 
 
 def grow(packed):
-    power = inverse(packed[:, -8:-7, :1].astype(F32))
+    power = inverse(packed[:, -8:-7, :].astype(F32))
     return packed[:, :-8].astype(F32) * power
 
 
@@ -254,11 +267,16 @@
     summed = lax.psum_scatter(partial, "filter", scatter_dimension=0, tiled=True)
     outputs = summed.astype(BF16).reshape(cotangent.shape)
     gathered = lax.all_gather(both.astype(F16), "filter", axis=0).astype(BF16)
-    theirs_grad, theirs_turned, mine_whole = weight_first(scale, share, patches, gathered)
-    received = lax.ppermute(theirs_grad, "core", [(0, 1), (1, 0)])
-    mine_grad, mine_turned = weight_second(scale, share, mine_whole, patches)
-    packed = shrink(mine_grad + received)
-    input_grad = input_gradient(width, share, core, theirs_turned, mine_turned, weights)
+    swap = [(0, 1), (1, 0)]
+    early, early_turned, theirs, mine = weight_first(scale, share, patches, gathered)
+    early = lax.ppermute(early, "core", swap)
+    late, late_turned = weight_second(scale, share, theirs, patches, 2, 1)
+    late = lax.ppermute(late, "core", swap)
+    mine_grad, mine_turned = weight_second(scale, share, mine, patches, 1, 0)
+    packed = shrink(mine_grad + jnp.concatenate([early, late], axis=0))
+    input_grad = input_gradient(
+        width, share, core, early_turned, late_turned, mine_turned, weights
+    )
     input_grad = input_grad.reshape(inputs.shape)
 
     packed = lax.all_to_all(packed, "chip", 0, 0, tiled=True)

time: 109 us -> 108 us (level)
  waiting for transfers between devices: 13.1 us -> 10.4 us
  Pallas kernels: 16.5 us -> 17.8 us
    pallas_call x1 -> x2, Pallas kernels: 1.87 us -> 3.79 us  [weight_second(): pl.pallas_call(functools.partial(second_kernel, scale), out_shape=(jax.Sh...]
    ppermute x1 -> x2, waiting for transfers between devices: 2.27 us -> 0.37 us  [the longest x1 0.36 us: on_device(): late = lax.ppermute(late, 'core', swap)]
    ppermute x1 -> x2, starting transfers between devices: 5.32 us -> 5.27 us  [the longest x1 5.27 us: on_device(): early = lax.ppermute(early, 'core', swap)]
  transfers between devices with their start and end apart: 3 -> 4, of which waited for: 3 -> 3; matrix products, arithmetic and copies ran while one was open for 4% -> 4% of each run, Pallas kernels for 8% -> 9%
where the time goes in v2:
time: 108 us
  blocking collectives  43.5 us (40%)
  Pallas kernels  17.8 us (16%)
  between operations  14.1 us (13%)
  starting transfers between devices  12.5 us (12%)
  waiting for transfers between devices  10.4 us (10%)
  other arithmetic  7.26 us (7%)
  local copies, waits for them, and re-layouts  2.14 us (2%)
    all_gather x1, blocking collectives, on_device(): gathered = lax.all_gather(both.astype(F16), 'filter', axis=0).astype(BF16)  43.5 us
    pallas_call x1, Pallas kernels, forward_partial(): pl.pallas_call(functools.partial(forward_kernel, width, share), out_shape...  7.88 us
    reduce_scatter x1, waiting for transfers between devices, on_device(): lax.psum_scatter(partial, 'filter', scatter_dimension=0, tiled=True)  7.16 us
    all_to_all x1, starting transfers between devices, on_device(): packed = lax.all_to_all(packed, 'chip', 0, 0, tiled=True)  7.15 us
    ppermute x1, starting transfers between devices, on_device(): early = lax.ppermute(early, 'core', swap)  5.27 us
    pallas_call x1, Pallas kernels, input_gradient(): pl.pallas_call(functools.partial(input_kernel, width, share), out_shape=j...  4.57 us
    pallas_call x2, Pallas kernels, weight_second(): pl.pallas_call(functools.partial(second_kernel, scale), out_shape=(jax.Sh...  3.79 us
    all_to_all x1, waiting for transfers between devices, on_device(): packed = lax.all_to_all(packed, 'chip', 0, 0, tiled=True)  2.81 us
  transfers between devices with their start and end apart: 4, of which 3 were waited for; matrix products, arithmetic and copies ran while one was open for 4% of the time, Pallas kernels for 9%

profile of v2, /device:TPU:1, one launch (start us, length us, event | category | flops | bytes accessed | tf_op | source)
XLA Modules:
  0.0 107.7 jit_solution(11401283754562895509)
XLA Ops:
  7.2 0.0 reduce-scatter.2.cloned.1.call-start
  7.2 7.9 %forward.1 = (f32[1152,1024]{1,0:T(8,128)}, f32[296,512]{1,0:T(8,128)S(1)}, bf16[1152,1152]{1,0:T(8,128)(2,1)S(1)}) custom-call(s32[1]{0:T(128)} %bitcast.core_ref, bf16[1152,128]{1,0:T(8,128)(2,1)} %bitcast.16, bf16[144,1024]{1,0:T(8,128)(2,1)} %bitcast.17, bf16[1152,1024]{1,0:T(8,128)(2,1)} %bitcast.14), custom_call_target="tpu_custom_call" | custom-call | tf_op jit(solution)/shard_map/forward/pallas_call | solution.py:95
  15.1 0.0 reduce-scatter.2.cloned.1.call-update
  15.2 43.5 %all-gather.2 = f16[2368,512]{1,0:T(8,128)(2,1)S(1)} all-gather(f16[296,512]{1,0:T(8,128)(2,1)S(1)} %convert_element_type.20), channel_id=2, replica_groups=mesh['chip'=16,'core'=2,'filter'=8] {'filter'}, dimensions={0}, use_global_device_ids=true | all-gather | bytes 2727936 | tf_op jit(solution)/shard_map/all_gather | solution.py:269
  58.7 0.5 convert_element_type.26
  59.2 1.6 %weight_first.1 = (f32[8,288,128]{2,1,0:T(8,128)S(1)}, bf16[256,1152]{1,0:T(8,128)(2,1)}, bf16[1152,512]{1,0:T(8,128)(2,1)S(1)}, bf16[1152,512]{1,0:T(8,128)(2,1)S(1)}) custom-call(bf16[1152,1152]{1,0:T(8,128)(2,1)S(1)} %get-tuple-element.16.patch_ref, bf16[8,296,512]{2,1,0:T(8,128)(2,1)S(1)} %bitcast.13), custom_call_target="tpu_custom_call" | custom-call | tf_op jit(solution)/shard_map/weight_first/pallas_call | solution.py:150
  60.8 5.3 %collective-permute-start = (f32[8,288,128]{2,1,0:T(8,128)S(1)}, f32[8,288,128]{2,1,0:T(8,128)S(1)}, u32[]{:S(2)}, u32[]{:S(2)}) collective-permute-start(f32[8,288,128]{2,1,0:T(8,128)S(1)} %get-tuple-element.20), channel_id=1, source_target_pairs={{0,8},{8,0},{1,9},{9,1},{2,10},{10,2},{3,11},{11,3},{4,12},{12,4},... | collective-permute-start | bytes 3538952 | tf_op jit(solution)/shard_map/ppermute | solution.py:272
  66.1 1.2 %weight_second.3 = (f32[8,288,128]{2,1,0:T(8,128)S(1)}, bf16[256,1152]{1,0:T(8,128)(2,1)}) custom-call(bf16[1152,512]{1,0:T(8,128)(2,1)S(1)} %get-tuple-element.21.cot_ref, bf16[1152,1152]{1,0:T(8,128)(2,1)S(1)} %get-tuple-element.16.patch_ref), custom_call_target="tpu_custom_call" | custom-call | tf_op jit(solution)/shard_map/weight_second/pallas_call | solution.py:174
  67.2 0.0 collective-permute-start.1
  67.2 2.6 %weight_second.2 = (f32[16,288,128]{2,1,0:T(8,128)S(1)}, bf16[512,1152]{1,0:T(8,128)(2,1)}) custom-call(bf16[1152,512]{1,0:T(8,128)(2,1)S(1)} %get-tuple-element.18.cot_ref, bf16[1152,1152]{1,0:T(8,128)(2,1)S(1)} %get-tuple-element.16.patch_ref), custom_call_target="tpu_custom_call" | custom-call | tf_op jit(solution)/shard_map/weight_second/pallas_call | solution.py:174
  69.8 0.0 collective-permute-done
  69.9 0.4 collective-permute-done.1
  70.2 0.4 abs_reduce_fusion
  70.6 0.0 copy-start
  70.7 1.5 %select_convert_fusion = f16[16,296,128]{2,1,0:T(8,128)(2,1)} fusion(f32[16,288,128]{2,1,0:T(8,128)S(1)} %get-tuple-element.30, f32[16]{0:T(128)S(1)} %get-tuple-element.32, f32[16]{0:T(128)S(1)} %get-tuple-element.31, pred[296]{0:T(512)(128)(4,1)S(1)} %iota_compare_fusion), kind=kLoop, calls=%fused_computation | loop fusion | flops 1818624 | bytes 3572136 | tf_op jit(solution)/shard_map/convert_element_type | solution.py:243
  72.2 7.2 %all-to-all-start = ((f16[16,296,128]{2,1,0:T(8,128)(2,1)}), f16[16,296,128]{2,1,0:T(8,128)(2,1)}, u32[]{:S(2)}, u32[]{:S(2)}) async-start(f16[16,296,128]{2,1,0:T(8,128)(2,1)} %select_convert_fusion), calls=%async_computation | async-start | bytes 2424832 | tf_op jit(solution)/shard_map/all_to_all | solution.py:282
  79.3 1.1 copy-done.2
  80.4 1.1 copy-done.3
  81.5 4.6 %input_grad.1 = bf16[1152,128]{1,0:T(8,128)(2,1)} custom-call(s32[1]{0:T(128)} %bitcast.core_ref, bf16[256,1152]{1,0:T(8,128)(2,1)S(1)} %copy-done.2, bf16[256,1152]{1,0:T(8,128)(2,1)S(1)} %copy-done.3, bf16[512,1152]{1,0:T(8,128)(2,1)S(1)} %copy-done.1, bf16[1152,1024]{1,0:T(8,128)(2,1)S(1)} %bitcast.15), custom_call_target="tpu_custom_call" | custom-call | tf_op jit(solution)/shard_map/input_grad/pallas_call | solution.py:227
  86.0 7.2 %reduce-scatter.2.cloned.1.call-done = f32[144,1024]{1,0:T(8,128)} async-done(((f32[1152,1024]{1,0:T(8,128)}), f32[144,1024]{1,0:T(8,128)}) %reduce-scatter.2.cloned.1.call-update) | async-done | bytes 589840 | tf_op jit(solution)/shard_map/reduce_scatter | solution.py:267
  93.2 1.8 %convert_element_type.23 = bf16[144,1024]{1,0:T(8,128)(2,1)} convert(f32[144,1024]{1,0:T(8,128)} %reduce-scatter.2.cloned.1.call-done) | non-fusion elementwise | flops 147456 | bytes 884736 | tf_op jit(solution)/shard_map/convert_element_type | solution.py:268
  95.0 2.8 %all-to-all-done = f16[16,296,128]{2,1,0:T(8,128)(2,1)} async-done(((f16[16,296,128]{2,1,0:T(8,128)(2,1)}), f16[16,296,128]{2,1,0:T(8,128)(2,1)}, u32[]{:S(2)}, u32[]{:S(2)}) %all-to-all-start) | async-done | bytes 1212448 | tf_op jit(solution)/shard_map/all_to_all | solution.py:282
  97.8 0.8 fusion.6
  98.7 2.2 %multiply_reduce_fusion = f32[288,128]{1,0:T(8,128)} fusion(f32[16,128]{1,0:T(8,128)S(1)} %bitcast.21, f16[16,296,128]{2,1,0:T(8,128)(2,1)} %all-to-all-done), kind=kLoop, calls=%fused_computation.2 | loop fusion | flops 1732608 | bytes 1335296 | tf_op jit(solution)/shard_map/reduce_sum | solution.py:284
  (8 shorter events, 0.1 us)
Async XLA Ops:
  7.2 86.0 %reduce-scatter.2.cloned.1.call-start = ((), (), s32[]{:S(2)}) async-start(), calls=%async_computation.2 | async-start | bytes 5308416 | tf_op jit(solution)/shard_map/reduce_scatter | solution.py:267
  60.8 9.1 %collective-permute-start = (f32[8,288,128]{2,1,0:T(8,128)S(1)}, f32[8,288,128]{2,1,0:T(8,128)S(1)}, u32[]{:S(2)}, u32[]{:S(2)}) collective-permute-start(f32[8,288,128]{2,1,0:T(8,128)S(1)} %get-tuple-element.20), channel_id=1, source_target_pairs={{0,8},{8,0},{1,9},{9,1},{2,10},{10,2},{3,11},{11,3},{4,12},{12,4},... | collective-permute-start | bytes 3538952 | tf_op jit(solution)/shard_map/ppermute | solution.py:272
  67.2 3.0 %collective-permute-start.1 = (f32[8,288,128]{2,1,0:T(8,128)S(1)}, f32[8,288,128]{2,1,0:T(8,128)S(1)}, u32[]{:S(2)}, u32[]{:S(2)}) collective-permute-start(f32[8,288,128]{2,1,0:T(8,128)S(1)} %get-tuple-element.22), channel_id=1, source_target_pairs={{0,8},{8,0},{1,9},{9,1},{2,10},{10,2},{3,11},{11,3},{4,12},{12,4},... | collective-permute-start | bytes 3538952 | tf_op jit(solution)/shard_map/ppermute | solution.py:274
  70.6 8.7 %copy-start = (bf16[3,3,128,1024]{3,2,1,0:T(8,128)(2,1)S(1)}, bf16[3,3,128,1024]{3,2,1,0:T(8,128)(2,1)}, u32[]{:S(2)}) copy-start(bf16[3,3,128,1024]{3,2,1,0:T(8,128)(2,1)} %param.4) | copy-start | bytes 7077892
  70.6 8.7 %copy-start.1 = (bf16[512,1152]{1,0:T(8,128)(2,1)S(1)}, bf16[512,1152]{1,0:T(8,128)(2,1)}, u32[]{:S(2)}) copy-start(bf16[512,1152]{1,0:T(8,128)(2,1)} %get-tuple-element.27.refs_2_) | copy-start | bytes 3538948
  72.2 25.7 %all-to-all-start = ((f16[16,296,128]{2,1,0:T(8,128)(2,1)}), f16[16,296,128]{2,1,0:T(8,128)(2,1)}, u32[]{:S(2)}, u32[]{:S(2)}) async-start(f16[16,296,128]{2,1,0:T(8,128)(2,1)} %select_convert_fusion), calls=%async_computation | async-start | bytes 2424832 | tf_op jit(solution)/shard_map/all_to_all | solution.py:282
  79.3 1.1 copy-start.2
  80.4 1.1 copy-start.3
Sparse Core Ops, SparseCore 0:
  15.2 77.9 reduce-scatter.1

commit v3 on v2

--- a/solution.py
+++ b/solution.py
@@ -88,7 +88,7 @@
     cells, chans = x.shape
     taps, channels = weights.shape
     rows = 2 * cot.shape[0] + 8
-    block = channels // 4
+    block = channels // 2
     x = pltpu.with_memory_space_constraint(x, pltpu.HBM)
     cot = pltpu.with_memory_space_constraint(cot, pltpu.HBM)
     weights = pltpu.with_memory_space_constraint(weights, pltpu.HBM)
@@ -99,7 +99,7 @@
             jax.ShapeDtypeStruct((rows, channels // 2), F32),
             jax.ShapeDtypeStruct((cells, taps), BF16),
         ),
-        grid=(4,),
+        grid=(2,),
         in_specs=[
             pl.BlockSpec(memory_space=pltpu.SMEM),
             pl.BlockSpec((cells, chans), lambda i: (0, 0)),

time: 108 us -> 108 us (level)
  no operation moved by 1% of the time
where the time goes in v3:
time: 108 us; the launch traced here: 107 us
  blocking collectives  43.5 us (40%)
  Pallas kernels  17.5 us (16%)
  between operations  14.1 us (13%)
  starting transfers between devices  12.5 us (12%)
  waiting for transfers between devices  10.4 us (10%)
  other arithmetic  7.26 us (7%)
  local copies, waits for them, and re-layouts  2.14 us (2%)
    all_gather x1, blocking collectives, on_device(): gathered = lax.all_gather(both.astype(F16), 'filter', axis=0).astype(BF16)  43.5 us
    pallas_call x1, Pallas kernels, forward_partial(): pl.pallas_call(functools.partial(forward_kernel, width, share), out_shape...  7.5 us
    all_to_all x1, starting transfers between devices, on_device(): packed = lax.all_to_all(packed, 'chip', 0, 0, tiled=True)  7.17 us
    reduce_scatter x1, waiting for transfers between devices, on_device(): lax.psum_scatter(partial, 'filter', scatter_dimension=0, tiled=True)  7.16 us
    ppermute x1, starting transfers between devices, on_device(): early = lax.ppermute(early, 'core', swap)  5.25 us
    pallas_call x1, Pallas kernels, input_gradient(): pl.pallas_call(functools.partial(input_kernel, width, share), out_shape=j...  4.56 us
    pallas_call x2, Pallas kernels, weight_second(): pl.pallas_call(functools.partial(second_kernel, scale), out_shape=(jax.Sh...  3.78 us
    all_to_all x1, waiting for transfers between devices, on_device(): packed = lax.all_to_all(packed, 'chip', 0, 0, tiled=True)  2.81 us
  transfers between devices with their start and end apart: 4, of which 3 were waited for; matrix products, arithmetic and copies ran while one was open for 4% of the time, Pallas kernels for 9%

profile of v3, /device:TPU:1, one launch (start us, length us, event | category | flops | bytes accessed | tf_op | source)
XLA Modules:
  0.0 107.3 jit_solution(8672161042956931255)
XLA Ops:
  7.2 0.0 reduce-scatter.2.cloned.1.call-start
  7.2 7.5 %forward.1 = (f32[1152,1024]{1,0:T(8,128)}, f32[296,512]{1,0:T(8,128)S(1)}, bf16[1152,1152]{1,0:T(8,128)(2,1)S(1)}) custom-call(s32[1]{0:T(128)} %bitcast.core_ref, bf16[1152,128]{1,0:T(8,128)(2,1)} %bitcast.16, bf16[144,1024]{1,0:T(8,128)(2,1)} %bitcast.17, bf16[1152,1024]{1,0:T(8,128)(2,1)} %bitcast.14), custom_call_target="tpu_custom_call" | custom-call | tf_op jit(solution)/shard_map/forward/pallas_call | solution.py:95
  14.7 0.0 reduce-scatter.2.cloned.1.call-update
  14.8 43.5 %all-gather.2 = f16[2368,512]{1,0:T(8,128)(2,1)S(1)} all-gather(f16[296,512]{1,0:T(8,128)(2,1)S(1)} %convert_element_type.20), channel_id=2, replica_groups=mesh['chip'=16,'core'=2,'filter'=8] {'filter'}, dimensions={0}, use_global_device_ids=true | all-gather | bytes 2727936 | tf_op jit(solution)/shard_map/all_gather | solution.py:269
  58.3 0.5 convert_element_type.26
  58.8 1.6 %weight_first.1 = (f32[8,288,128]{2,1,0:T(8,128)S(1)}, bf16[256,1152]{1,0:T(8,128)(2,1)}, bf16[1152,512]{1,0:T(8,128)(2,1)S(1)}, bf16[1152,512]{1,0:T(8,128)(2,1)S(1)}) custom-call(bf16[1152,1152]{1,0:T(8,128)(2,1)S(1)} %get-tuple-element.16.patch_ref, bf16[8,296,512]{2,1,0:T(8,128)(2,1)S(1)} %bitcast.13), custom_call_target="tpu_custom_call" | custom-call | tf_op jit(solution)/shard_map/weight_first/pallas_call | solution.py:150
  60.4 5.2 %collective-permute-start = (f32[8,288,128]{2,1,0:T(8,128)S(1)}, f32[8,288,128]{2,1,0:T(8,128)S(1)}, u32[]{:S(2)}, u32[]{:S(2)}) collective-permute-start(f32[8,288,128]{2,1,0:T(8,128)S(1)} %get-tuple-element.20), channel_id=1, source_target_pairs={{0,8},{8,0},{1,9},{9,1},{2,10},{10,2},{3,11},{11,3},{4,12},{12,4},... | collective-permute-start | bytes 3538952 | tf_op jit(solution)/shard_map/ppermute | solution.py:272
  65.7 1.2 %weight_second.3 = (f32[8,288,128]{2,1,0:T(8,128)S(1)}, bf16[256,1152]{1,0:T(8,128)(2,1)}) custom-call(bf16[1152,512]{1,0:T(8,128)(2,1)S(1)} %get-tuple-element.21.cot_ref, bf16[1152,1152]{1,0:T(8,128)(2,1)S(1)} %get-tuple-element.16.patch_ref), custom_call_target="tpu_custom_call" | custom-call | tf_op jit(solution)/shard_map/weight_second/pallas_call | solution.py:174
  66.8 0.0 collective-permute-start.1
  66.8 2.6 %weight_second.2 = (f32[16,288,128]{2,1,0:T(8,128)S(1)}, bf16[512,1152]{1,0:T(8,128)(2,1)}) custom-call(bf16[1152,512]{1,0:T(8,128)(2,1)S(1)} %get-tuple-element.18.cot_ref, bf16[1152,1152]{1,0:T(8,128)(2,1)S(1)} %get-tuple-element.16.patch_ref), custom_call_target="tpu_custom_call" | custom-call | tf_op jit(solution)/shard_map/weight_second/pallas_call | solution.py:174
  69.4 0.0 collective-permute-done
  69.5 0.4 collective-permute-done.1
  69.8 0.4 abs_reduce_fusion
  70.2 0.0 copy-start
  70.3 1.5 %select_convert_fusion = f16[16,296,128]{2,1,0:T(8,128)(2,1)} fusion(f32[16,288,128]{2,1,0:T(8,128)S(1)} %get-tuple-element.30, f32[16]{0:T(128)S(1)} %get-tuple-element.32, f32[16]{0:T(128)S(1)} %get-tuple-element.31, pred[296]{0:T(512)(128)(4,1)S(1)} %iota_compare_fusion), kind=kLoop, calls=%fused_computation | loop fusion | flops 1818624 | bytes 3572136 | tf_op jit(solution)/shard_map/convert_element_type | solution.py:243
  71.8 7.2 %all-to-all-start = ((f16[16,296,128]{2,1,0:T(8,128)(2,1)}), f16[16,296,128]{2,1,0:T(8,128)(2,1)}, u32[]{:S(2)}, u32[]{:S(2)}) async-start(f16[16,296,128]{2,1,0:T(8,128)(2,1)} %select_convert_fusion), calls=%async_computation | async-start | bytes 2424832 | tf_op jit(solution)/shard_map/all_to_all | solution.py:282
  79.0 1.1 copy-done.2
  80.0 1.1 %copy-done.3 = bf16[256,1152]{1,0:T(8,128)(2,1)S(1)} copy-done((bf16[256,1152]{1,0:T(8,128)(2,1)S(1)}, bf16[256,1152]{1,0:T(8,128)(2,1)}, u32[]{:S(2)}) %copy-start.3) | copy-done | bytes 589848
  81.1 4.6 %input_grad.1 = bf16[1152,128]{1,0:T(8,128)(2,1)} custom-call(s32[1]{0:T(128)} %bitcast.core_ref, bf16[256,1152]{1,0:T(8,128)(2,1)S(1)} %copy-done.2, bf16[256,1152]{1,0:T(8,128)(2,1)S(1)} %copy-done.3, bf16[512,1152]{1,0:T(8,128)(2,1)S(1)} %copy-done.1, bf16[1152,1024]{1,0:T(8,128)(2,1)S(1)} %bitcast.15), custom_call_target="tpu_custom_call" | custom-call | tf_op jit(solution)/shard_map/input_grad/pallas_call | solution.py:227
  85.7 7.2 %reduce-scatter.2.cloned.1.call-done = f32[144,1024]{1,0:T(8,128)} async-done(((f32[1152,1024]{1,0:T(8,128)}), f32[144,1024]{1,0:T(8,128)}) %reduce-scatter.2.cloned.1.call-update) | async-done | bytes 589840 | tf_op jit(solution)/shard_map/reduce_scatter | solution.py:267
  92.8 1.8 %convert_element_type.23 = bf16[144,1024]{1,0:T(8,128)(2,1)} convert(f32[144,1024]{1,0:T(8,128)} %reduce-scatter.2.cloned.1.call-done) | non-fusion elementwise | flops 147456 | bytes 884736 | tf_op jit(solution)/shard_map/convert_element_type | solution.py:268
  94.6 2.8 %all-to-all-done = f16[16,296,128]{2,1,0:T(8,128)(2,1)} async-done(((f16[16,296,128]{2,1,0:T(8,128)(2,1)}), f16[16,296,128]{2,1,0:T(8,128)(2,1)}, u32[]{:S(2)}, u32[]{:S(2)}) %all-to-all-start) | async-done | bytes 1212448 | tf_op jit(solution)/shard_map/all_to_all | solution.py:282
  97.5 0.8 fusion.6
  98.3 2.2 %multiply_reduce_fusion = f32[288,128]{1,0:T(8,128)} fusion(f32[16,128]{1,0:T(8,128)S(1)} %bitcast.21, f16[16,296,128]{2,1,0:T(8,128)(2,1)} %all-to-all-done), kind=kLoop, calls=%fused_computation.2 | loop fusion | flops 1732608 | bytes 1335296 | tf_op jit(solution)/shard_map/reduce_sum | solution.py:284
  (8 shorter events, 0.1 us)
Async XLA Ops:
  7.2 85.7 %reduce-scatter.2.cloned.1.call-start = ((), (), s32[]{:S(2)}) async-start(), calls=%async_computation.2 | async-start | bytes 5308416 | tf_op jit(solution)/shard_map/reduce_scatter | solution.py:267
  60.4 9.0 %collective-permute-start = (f32[8,288,128]{2,1,0:T(8,128)S(1)}, f32[8,288,128]{2,1,0:T(8,128)S(1)}, u32[]{:S(2)}, u32[]{:S(2)}) collective-permute-start(f32[8,288,128]{2,1,0:T(8,128)S(1)} %get-tuple-element.20), channel_id=1, source_target_pairs={{0,8},{8,0},{1,9},{9,1},{2,10},{10,2},{3,11},{11,3},{4,12},{12,4},... | collective-permute-start | bytes 3538952 | tf_op jit(solution)/shard_map/ppermute | solution.py:272
  66.8 3.0 %collective-permute-start.1 = (f32[8,288,128]{2,1,0:T(8,128)S(1)}, f32[8,288,128]{2,1,0:T(8,128)S(1)}, u32[]{:S(2)}, u32[]{:S(2)}) collective-permute-start(f32[8,288,128]{2,1,0:T(8,128)S(1)} %get-tuple-element.22), channel_id=1, source_target_pairs={{0,8},{8,0},{1,9},{9,1},{2,10},{10,2},{3,11},{11,3},{4,12},{12,4},... | collective-permute-start | bytes 3538952 | tf_op jit(solution)/shard_map/ppermute | solution.py:274
  70.2 8.7 %copy-start = (bf16[3,3,128,1024]{3,2,1,0:T(8,128)(2,1)S(1)}, bf16[3,3,128,1024]{3,2,1,0:T(8,128)(2,1)}, u32[]{:S(2)}) copy-start(bf16[3,3,128,1024]{3,2,1,0:T(8,128)(2,1)} %param.4) | copy-start | bytes 7077892
  70.2 8.7 %copy-start.1 = (bf16[512,1152]{1,0:T(8,128)(2,1)S(1)}, bf16[512,1152]{1,0:T(8,128)(2,1)}, u32[]{:S(2)}) copy-start(bf16[512,1152]{1,0:T(8,128)(2,1)} %get-tuple-element.27.refs_2_) | copy-start | bytes 3538948
  71.8 25.7 %all-to-all-start = ((f16[16,296,128]{2,1,0:T(8,128)(2,1)}), f16[16,296,128]{2,1,0:T(8,128)(2,1)}, u32[]{:S(2)}, u32[]{:S(2)}) async-start(f16[16,296,128]{2,1,0:T(8,128)(2,1)} %select_convert_fusion), calls=%async_computation | async-start | bytes 2424832 | tf_op jit(solution)/shard_map/all_to_all | solution.py:282
  79.0 1.1 copy-start.2
  80.0 1.1 %copy-start.3 = (bf16[256,1152]{1,0:T(8,128)(2,1)S(1)}, bf16[256,1152]{1,0:T(8,128)(2,1)}, u32[]{:S(2)}) copy-start(bf16[256,1152]{1,0:T(8,128)(2,1)} %get-tuple-element.26.refs_1_) | copy-start | bytes 1769476
Sparse Core Ops, SparseCore 0:
  14.9 77.9 reduce-scatter.1

commit v4 on v3

--- a/solution.py
+++ b/solution.py
@@ -74,14 +74,19 @@
 
 
 def forward_kernel(width, share, core_ref, x_ref, cot_ref, kernel_ref, *refs):
-    out_ref, both_ref, patch_ref, pad_ref = refs
+    out_ref, both_ref, patch_ref, pad_ref, held_ref, sem = refs
+    block = out_ref.shape[1]
 
     @pl.when(pl.program_id(0) == 0)
     def _():
+        copy = pltpu.make_async_copy(kernel_ref, held_ref, sem)
+        copy.start()
         build_patches(width, x_ref, pad_ref, patch_ref)
         split_by_core(share, core_ref[0], cot_ref, both_ref)
-
-    out_ref[...] = jnp.dot(patch_ref[...], kernel_ref[...], preferred_element_type=F32)
+        copy.wait()
+
+    columns = pl.ds(pl.multiple_of(pl.program_id(0) * block, block), block)
+    out_ref[...] = jnp.dot(patch_ref[...], held_ref[:, columns], preferred_element_type=F32)
 
 
 def forward_partial(width, share, core, x, cot, weights):
@@ -104,15 +109,19 @@
             pl.BlockSpec(memory_space=pltpu.SMEM),
             pl.BlockSpec((cells, chans), lambda i: (0, 0)),
             pl.BlockSpec(cot.shape, lambda i: (0, 0)),
-            pl.BlockSpec((taps, block), lambda i: (0, i)),
+            pl.BlockSpec(memory_space=pl.ANY),
         ],
         out_specs=(
             pl.BlockSpec((cells, block), lambda i: (0, i)),
             pl.BlockSpec((rows, channels // 2), lambda i: (0, 0)),
             pl.BlockSpec((cells, taps), lambda i: (0, 0)),
         ),
-        scratch_shapes=[pltpu.VMEM((3, cells + 2 * width, chans), BF16)],
-        compiler_params=pltpu.CompilerParams(vmem_limit_bytes=24 << 20),
+        scratch_shapes=[
+            pltpu.VMEM((3, cells + 2 * width, chans), BF16),
+            pltpu.VMEM((taps, channels), BF16),
+            pltpu.SemaphoreType.DMA,
+        ],
+        compiler_params=pltpu.CompilerParams(vmem_limit_bytes=26 << 20),
         name="forward",
     )(core, x, cot, weights)
 

time: 108 us -> 108 us (level)
  no operation moved by 1% of the time
where the time goes in v4:
time: 108 us; the launch traced here: 107 us
  blocking collectives  43.5 us (40%)
  Pallas kernels  17.6 us (16%)
  between operations  14.1 us (13%)
  starting transfers between devices  12.5 us (12%)
  waiting for transfers between devices  10.4 us (10%)
  other arithmetic  7.26 us (7%)
  local copies, waits for them, and re-layouts  2.14 us (2%)
    all_gather x1, blocking collectives, on_device(): gathered = lax.all_gather(both.astype(F16), 'filter', axis=0).astype(BF16)  43.5 us
    pallas_call x1, Pallas kernels, forward_partial(): pl.pallas_call(functools.partial(forward_kernel, width, share), out_shape...  7.66 us
    all_to_all x1, starting transfers between devices, on_device(): packed = lax.all_to_all(packed, 'chip', 0, 0, tiled=True)  7.21 us
    reduce_scatter x1, waiting for transfers between devices, on_device(): lax.psum_scatter(partial, 'filter', scatter_dimension=0, tiled=True)  7.19 us
    ppermute x1, starting transfers between devices, on_device(): early = lax.ppermute(early, 'core', swap)  5.2 us
    pallas_call x1, Pallas kernels, input_gradient(): pl.pallas_call(functools.partial(input_kernel, width, share), out_shape=j...  4.56 us
    pallas_call x2, Pallas kernels, weight_second(): pl.pallas_call(functools.partial(second_kernel, scale), out_shape=(jax.Sh...  3.78 us
    all_to_all x1, waiting for transfers between devices, on_device(): packed = lax.all_to_all(packed, 'chip', 0, 0, tiled=True)  2.79 us
  transfers between devices with their start and end apart: 4, of which 3 were waited for; matrix products, arithmetic and copies ran while one was open for 4% of the time, Pallas kernels for 9%

profile of v4, /device:TPU:1, one launch (start us, length us, event | category | flops | bytes accessed | tf_op | source)
XLA Modules:
  0.0 107.5 jit_solution(10371947980169527162)
XLA Ops:
  7.2 0.0 reduce-scatter.2.cloned.1.call-start
  7.2 7.7 %forward.1 = (f32[1152,1024]{1,0:T(8,128)}, f32[296,512]{1,0:T(8,128)S(1)}, bf16[1152,1152]{1,0:T(8,128)(2,1)S(1)}) custom-call(s32[1]{0:T(128)} %bitcast.core_ref, bf16[1152,128]{1,0:T(8,128)(2,1)} %bitcast.16, bf16[144,1024]{1,0:T(8,128)(2,1)} %bitcast.17, bf16[1152,1024]{1,0:T(8,128)(2,1)} %bitcast.14), custom_call_target="tpu_custom_call" | custom-call | tf_op jit(solution)/shard_map/forward/pallas_call | solution.py:100
  14.9 0.0 reduce-scatter.2.cloned.1.call-update
  15.0 43.5 %all-gather.2 = f16[2368,512]{1,0:T(8,128)(2,1)S(1)} all-gather(f16[296,512]{1,0:T(8,128)(2,1)S(1)} %convert_element_type.20), channel_id=2, replica_groups=mesh['chip'=16,'core'=2,'filter'=8] {'filter'}, dimensions={0}, use_global_device_ids=true | all-gather | bytes 2727936 | tf_op jit(solution)/shard_map/all_gather | solution.py:278
  58.5 0.5 convert_element_type.26
  58.9 1.6 %weight_first.1 = (f32[8,288,128]{2,1,0:T(8,128)S(1)}, bf16[256,1152]{1,0:T(8,128)(2,1)}, bf16[1152,512]{1,0:T(8,128)(2,1)S(1)}, bf16[1152,512]{1,0:T(8,128)(2,1)S(1)}) custom-call(bf16[1152,1152]{1,0:T(8,128)(2,1)S(1)} %get-tuple-element.16.patch_ref, bf16[8,296,512]{2,1,0:T(8,128)(2,1)S(1)} %bitcast.13), custom_call_target="tpu_custom_call" | custom-call | tf_op jit(solution)/shard_map/weight_first/pallas_call | solution.py:159
  60.6 5.2 %collective-permute-start = (f32[8,288,128]{2,1,0:T(8,128)S(1)}, f32[8,288,128]{2,1,0:T(8,128)S(1)}, u32[]{:S(2)}, u32[]{:S(2)}) collective-permute-start(f32[8,288,128]{2,1,0:T(8,128)S(1)} %get-tuple-element.20), channel_id=1, source_target_pairs={{0,8},{8,0},{1,9},{9,1},{2,10},{10,2},{3,11},{11,3},{4,12},{12,4},... | collective-permute-start | bytes 3538952 | tf_op jit(solution)/shard_map/ppermute | solution.py:281
  65.8 1.2 %weight_second.3 = (f32[8,288,128]{2,1,0:T(8,128)S(1)}, bf16[256,1152]{1,0:T(8,128)(2,1)}) custom-call(bf16[1152,512]{1,0:T(8,128)(2,1)S(1)} %get-tuple-element.21.cot_ref, bf16[1152,1152]{1,0:T(8,128)(2,1)S(1)} %get-tuple-element.16.patch_ref), custom_call_target="tpu_custom_call" | custom-call | tf_op jit(solution)/shard_map/weight_second/pallas_call | solution.py:183
  66.9 0.0 collective-permute-start.1
  66.9 2.6 %weight_second.2 = (f32[16,288,128]{2,1,0:T(8,128)S(1)}, bf16[512,1152]{1,0:T(8,128)(2,1)}) custom-call(bf16[1152,512]{1,0:T(8,128)(2,1)S(1)} %get-tuple-element.18.cot_ref, bf16[1152,1152]{1,0:T(8,128)(2,1)S(1)} %get-tuple-element.16.patch_ref), custom_call_target="tpu_custom_call" | custom-call | tf_op jit(solution)/shard_map/weight_second/pallas_call | solution.py:183
  69.6 0.0 collective-permute-done
  69.6 0.4 collective-permute-done.1
  69.9 0.4 abs_reduce_fusion
  70.3 0.0 copy-start
  70.4 1.5 %select_convert_fusion = f16[16,296,128]{2,1,0:T(8,128)(2,1)} fusion(f32[16,288,128]{2,1,0:T(8,128)S(1)} %get-tuple-element.30, f32[16]{0:T(128)S(1)} %get-tuple-element.32, f32[16]{0:T(128)S(1)} %get-tuple-element.31, pred[296]{0:T(512)(128)(4,1)S(1)} %iota_compare_fusion), kind=kLoop, calls=%fused_computation | loop fusion | flops 1818624 | bytes 3572136 | tf_op jit(solution)/shard_map/convert_element_type | solution.py:252
  71.9 7.2 %all-to-all-start = ((f16[16,296,128]{2,1,0:T(8,128)(2,1)}), f16[16,296,128]{2,1,0:T(8,128)(2,1)}, u32[]{:S(2)}, u32[]{:S(2)}) async-start(f16[16,296,128]{2,1,0:T(8,128)(2,1)} %select_convert_fusion), calls=%async_computation | async-start | bytes 2424832 | tf_op jit(solution)/shard_map/all_to_all | solution.py:291
  79.1 1.1 copy-done.2
  80.2 1.1 copy-done.3
  81.2 4.6 %input_grad.1 = bf16[1152,128]{1,0:T(8,128)(2,1)} custom-call(s32[1]{0:T(128)} %bitcast.core_ref, bf16[256,1152]{1,0:T(8,128)(2,1)S(1)} %copy-done.2, bf16[256,1152]{1,0:T(8,128)(2,1)S(1)} %copy-done.3, bf16[512,1152]{1,0:T(8,128)(2,1)S(1)} %copy-done.1, bf16[1152,1024]{1,0:T(8,128)(2,1)S(1)} %bitcast.15), custom_call_target="tpu_custom_call" | custom-call | tf_op jit(solution)/shard_map/input_grad/pallas_call | solution.py:236
  85.8 7.2 %reduce-scatter.2.cloned.1.call-done = f32[144,1024]{1,0:T(8,128)} async-done(((f32[1152,1024]{1,0:T(8,128)}), f32[144,1024]{1,0:T(8,128)}) %reduce-scatter.2.cloned.1.call-update) | async-done | bytes 589840 | tf_op jit(solution)/shard_map/reduce_scatter | solution.py:276
  93.0 1.8 %convert_element_type.23 = bf16[144,1024]{1,0:T(8,128)(2,1)} convert(f32[144,1024]{1,0:T(8,128)} %reduce-scatter.2.cloned.1.call-done) | non-fusion elementwise | flops 147456 | bytes 884736 | tf_op jit(solution)/shard_map/convert_element_type | solution.py:277
  94.8 2.8 %all-to-all-done = f16[16,296,128]{2,1,0:T(8,128)(2,1)} async-done(((f16[16,296,128]{2,1,0:T(8,128)(2,1)}), f16[16,296,128]{2,1,0:T(8,128)(2,1)}, u32[]{:S(2)}, u32[]{:S(2)}) %all-to-all-start) | async-done | bytes 1212448 | tf_op jit(solution)/shard_map/all_to_all | solution.py:291
  97.6 0.8 fusion.6
  98.4 2.2 %multiply_reduce_fusion = f32[288,128]{1,0:T(8,128)} fusion(f32[16,128]{1,0:T(8,128)S(1)} %bitcast.21, f16[16,296,128]{2,1,0:T(8,128)(2,1)} %all-to-all-done), kind=kLoop, calls=%fused_computation.2 | loop fusion | flops 1732608 | bytes 1335296 | tf_op jit(solution)/shard_map/reduce_sum | solution.py:293
  (8 shorter events, 0.1 us)
Async XLA Ops:
  7.2 85.8 %reduce-scatter.2.cloned.1.call-start = ((), (), s32[]{:S(2)}) async-start(), calls=%async_computation.2 | async-start | bytes 5308416 | tf_op jit(solution)/shard_map/reduce_scatter | solution.py:276
  60.6 9.0 %collective-permute-start = (f32[8,288,128]{2,1,0:T(8,128)S(1)}, f32[8,288,128]{2,1,0:T(8,128)S(1)}, u32[]{:S(2)}, u32[]{:S(2)}) collective-permute-start(f32[8,288,128]{2,1,0:T(8,128)S(1)} %get-tuple-element.20), channel_id=1, source_target_pairs={{0,8},{8,0},{1,9},{9,1},{2,10},{10,2},{3,11},{11,3},{4,12},{12,4},... | collective-permute-start | bytes 3538952 | tf_op jit(solution)/shard_map/ppermute | solution.py:281
  66.9 3.0 %collective-permute-start.1 = (f32[8,288,128]{2,1,0:T(8,128)S(1)}, f32[8,288,128]{2,1,0:T(8,128)S(1)}, u32[]{:S(2)}, u32[]{:S(2)}) collective-permute-start(f32[8,288,128]{2,1,0:T(8,128)S(1)} %get-tuple-element.22), channel_id=1, source_target_pairs={{0,8},{8,0},{1,9},{9,1},{2,10},{10,2},{3,11},{11,3},{4,12},{12,4},... | collective-permute-start | bytes 3538952 | tf_op jit(solution)/shard_map/ppermute | solution.py:283
  70.3 8.7 %copy-start = (bf16[3,3,128,1024]{3,2,1,0:T(8,128)(2,1)S(1)}, bf16[3,3,128,1024]{3,2,1,0:T(8,128)(2,1)}, u32[]{:S(2)}) copy-start(bf16[3,3,128,1024]{3,2,1,0:T(8,128)(2,1)} %param.4) | copy-start | bytes 7077892
  70.4 8.7 %copy-start.1 = (bf16[512,1152]{1,0:T(8,128)(2,1)S(1)}, bf16[512,1152]{1,0:T(8,128)(2,1)}, u32[]{:S(2)}) copy-start(bf16[512,1152]{1,0:T(8,128)(2,1)} %get-tuple-element.27.refs_2_) | copy-start | bytes 3538948
  71.9 25.7 %all-to-all-start = ((f16[16,296,128]{2,1,0:T(8,128)(2,1)}), f16[16,296,128]{2,1,0:T(8,128)(2,1)}, u32[]{:S(2)}, u32[]{:S(2)}) async-start(f16[16,296,128]{2,1,0:T(8,128)(2,1)} %select_convert_fusion), calls=%async_computation | async-start | bytes 2424832 | tf_op jit(solution)/shard_map/all_to_all | solution.py:291
  79.1 1.1 copy-start.2
  80.2 1.1 %copy-start.3 = (bf16[256,1152]{1,0:T(8,128)(2,1)S(1)}, bf16[256,1152]{1,0:T(8,128)(2,1)}, u32[]{:S(2)}) copy-start(bf16[256,1152]{1,0:T(8,128)(2,1)} %get-tuple-element.26.refs_1_) | copy-start | bytes 1769476
Sparse Core Ops, SparseCore 0:
  15.0 77.9 reduce-scatter.1

commit v5 on v4

--- a/solution.py
+++ b/solution.py
@@ -93,7 +93,7 @@
     cells, chans = x.shape
     taps, channels = weights.shape
     rows = 2 * cot.shape[0] + 8
-    block = channels // 2
+    block = channels // 4
     x = pltpu.with_memory_space_constraint(x, pltpu.HBM)
     cot = pltpu.with_memory_space_constraint(cot, pltpu.HBM)
     weights = pltpu.with_memory_space_constraint(weights, pltpu.HBM)
@@ -104,7 +104,7 @@
             jax.ShapeDtypeStruct((rows, channels // 2), F32),
             jax.ShapeDtypeStruct((cells, taps), BF16),
         ),
-        grid=(2,),
+        grid=(4,),
         in_specs=[
             pl.BlockSpec(memory_space=pltpu.SMEM),
             pl.BlockSpec((cells, chans), lambda i: (0, 0)),

time: 108 us -> 108 us (level)
  no operation moved by 1% of the time
where the time goes in v5:
time: 108 us
  blocking collectives  43.5 us (40%)
  Pallas kernels  17.7 us (16%)
  between operations  14.1 us (13%)
  starting transfers between devices  12.5 us (12%)
  waiting for transfers between devices  10.4 us (10%)
  other arithmetic  7.26 us (7%)
  local copies, waits for them, and re-layouts  2.14 us (2%)
    all_gather x1, blocking collectives, on_device(): gathered = lax.all_gather(both.astype(F16), 'filter', axis=0).astype(BF16)  43.5 us
    pallas_call x1, Pallas kernels, forward_partial(): pl.pallas_call(functools.partial(forward_kernel, width, share), out_shape...  7.76 us
    reduce_scatter x1, waiting for transfers between devices, on_device(): lax.psum_scatter(partial, 'filter', scatter_dimension=0, tiled=True)  7.17 us
    all_to_all x1, starting transfers between devices, on_device(): packed = lax.all_to_all(packed, 'chip', 0, 0, tiled=True)  7.15 us
    ppermute x1, starting transfers between devices, on_device(): early = lax.ppermute(early, 'core', swap)  5.27 us
    pallas_call x1, Pallas kernels, input_gradient(): pl.pallas_call(functools.partial(input_kernel, width, share), out_shape=j...  4.56 us
    pallas_call x2, Pallas kernels, weight_second(): pl.pallas_call(functools.partial(second_kernel, scale), out_shape=(jax.Sh...  3.78 us
    all_to_all x1, waiting for transfers between devices, on_device(): packed = lax.all_to_all(packed, 'chip', 0, 0, tiled=True)  2.81 us
  transfers between devices with their start and end apart: 4, of which 3 were waited for; matrix products, arithmetic and copies ran while one was open for 4% of the time, Pallas kernels for 9%

profile of v5, /device:TPU:1, one launch (start us, length us, event | category | flops | bytes accessed | tf_op | source)
XLA Modules:
  0.0 107.6 jit_solution(18072926846495040339)
XLA Ops:
  7.2 0.0 reduce-scatter.2.cloned.1.call-start
  7.2 7.8 %forward.1 = (f32[1152,1024]{1,0:T(8,128)}, f32[296,512]{1,0:T(8,128)S(1)}, bf16[1152,1152]{1,0:T(8,128)(2,1)S(1)}) custom-call(s32[1]{0:T(128)} %bitcast.core_ref, bf16[1152,128]{1,0:T(8,128)(2,1)} %bitcast.16, bf16[144,1024]{1,0:T(8,128)(2,1)} %bitcast.17, bf16[1152,1024]{1,0:T(8,128)(2,1)} %bitcast.14), custom_call_target="tpu_custom_call" | custom-call | tf_op jit(solution)/shard_map/forward/pallas_call | solution.py:100
  15.0 0.0 reduce-scatter.2.cloned.1.call-update
  15.1 43.5 %all-gather.2 = f16[2368,512]{1,0:T(8,128)(2,1)S(1)} all-gather(f16[296,512]{1,0:T(8,128)(2,1)S(1)} %convert_element_type.20), channel_id=2, replica_groups=mesh['chip'=16,'core'=2,'filter'=8] {'filter'}, dimensions={0}, use_global_device_ids=true | all-gather | bytes 2727936 | tf_op jit(solution)/shard_map/all_gather | solution.py:278
  58.6 0.5 convert_element_type.26
  59.1 1.6 %weight_first.1 = (f32[8,288,128]{2,1,0:T(8,128)S(1)}, bf16[256,1152]{1,0:T(8,128)(2,1)}, bf16[1152,512]{1,0:T(8,128)(2,1)S(1)}, bf16[1152,512]{1,0:T(8,128)(2,1)S(1)}) custom-call(bf16[1152,1152]{1,0:T(8,128)(2,1)S(1)} %get-tuple-element.16.patch_ref, bf16[8,296,512]{2,1,0:T(8,128)(2,1)S(1)} %bitcast.13), custom_call_target="tpu_custom_call" | custom-call | tf_op jit(solution)/shard_map/weight_first/pallas_call | solution.py:159
  60.7 5.3 %collective-permute-start = (f32[8,288,128]{2,1,0:T(8,128)S(1)}, f32[8,288,128]{2,1,0:T(8,128)S(1)}, u32[]{:S(2)}, u32[]{:S(2)}) collective-permute-start(f32[8,288,128]{2,1,0:T(8,128)S(1)} %get-tuple-element.20), channel_id=1, source_target_pairs={{0,8},{8,0},{1,9},{9,1},{2,10},{10,2},{3,11},{11,3},{4,12},{12,4},... | collective-permute-start | bytes 3538952 | tf_op jit(solution)/shard_map/ppermute | solution.py:281
  66.0 1.2 %weight_second.3 = (f32[8,288,128]{2,1,0:T(8,128)S(1)}, bf16[256,1152]{1,0:T(8,128)(2,1)}) custom-call(bf16[1152,512]{1,0:T(8,128)(2,1)S(1)} %get-tuple-element.21.cot_ref, bf16[1152,1152]{1,0:T(8,128)(2,1)S(1)} %get-tuple-element.16.patch_ref), custom_call_target="tpu_custom_call" | custom-call | tf_op jit(solution)/shard_map/weight_second/pallas_call | solution.py:183
  67.1 0.0 collective-permute-start.1
  67.1 2.6 %weight_second.2 = (f32[16,288,128]{2,1,0:T(8,128)S(1)}, bf16[512,1152]{1,0:T(8,128)(2,1)}) custom-call(bf16[1152,512]{1,0:T(8,128)(2,1)S(1)} %get-tuple-element.18.cot_ref, bf16[1152,1152]{1,0:T(8,128)(2,1)S(1)} %get-tuple-element.16.patch_ref), custom_call_target="tpu_custom_call" | custom-call | tf_op jit(solution)/shard_map/weight_second/pallas_call | solution.py:183
  69.7 0.0 collective-permute-done
  69.7 0.4 collective-permute-done.1
  70.1 0.4 abs_reduce_fusion
  70.5 0.0 copy-start
  70.6 1.5 %select_convert_fusion = f16[16,296,128]{2,1,0:T(8,128)(2,1)} fusion(f32[16,288,128]{2,1,0:T(8,128)S(1)} %get-tuple-element.30, f32[16]{0:T(128)S(1)} %get-tuple-element.32, f32[16]{0:T(128)S(1)} %get-tuple-element.31, pred[296]{0:T(512)(128)(4,1)S(1)} %iota_compare_fusion), kind=kLoop, calls=%fused_computation | loop fusion | flops 1818624 | bytes 3572136 | tf_op jit(solution)/shard_map/convert_element_type | solution.py:252
  72.0 7.1 %all-to-all-start = ((f16[16,296,128]{2,1,0:T(8,128)(2,1)}), f16[16,296,128]{2,1,0:T(8,128)(2,1)}, u32[]{:S(2)}, u32[]{:S(2)}) async-start(f16[16,296,128]{2,1,0:T(8,128)(2,1)} %select_convert_fusion), calls=%async_computation | async-start | bytes 2424832 | tf_op jit(solution)/shard_map/all_to_all | solution.py:291
  79.2 1.1 copy-done.2
  80.3 1.1 copy-done.3
  81.4 4.6 %input_grad.1 = bf16[1152,128]{1,0:T(8,128)(2,1)} custom-call(s32[1]{0:T(128)} %bitcast.core_ref, bf16[256,1152]{1,0:T(8,128)(2,1)S(1)} %copy-done.2, bf16[256,1152]{1,0:T(8,128)(2,1)S(1)} %copy-done.3, bf16[512,1152]{1,0:T(8,128)(2,1)S(1)} %copy-done.1, bf16[1152,1024]{1,0:T(8,128)(2,1)S(1)} %bitcast.15), custom_call_target="tpu_custom_call" | custom-call | tf_op jit(solution)/shard_map/input_grad/pallas_call | solution.py:236
  85.9 7.2 %reduce-scatter.2.cloned.1.call-done = f32[144,1024]{1,0:T(8,128)} async-done(((f32[1152,1024]{1,0:T(8,128)}), f32[144,1024]{1,0:T(8,128)}) %reduce-scatter.2.cloned.1.call-update) | async-done | bytes 589840 | tf_op jit(solution)/shard_map/reduce_scatter | solution.py:276
  93.1 1.8 %convert_element_type.23 = bf16[144,1024]{1,0:T(8,128)(2,1)} convert(f32[144,1024]{1,0:T(8,128)} %reduce-scatter.2.cloned.1.call-done) | non-fusion elementwise | flops 147456 | bytes 884736 | tf_op jit(solution)/shard_map/convert_element_type | solution.py:277
  94.9 2.8 %all-to-all-done = f16[16,296,128]{2,1,0:T(8,128)(2,1)} async-done(((f16[16,296,128]{2,1,0:T(8,128)(2,1)}), f16[16,296,128]{2,1,0:T(8,128)(2,1)}, u32[]{:S(2)}, u32[]{:S(2)}) %all-to-all-start) | async-done | bytes 1212448 | tf_op jit(solution)/shard_map/all_to_all | solution.py:291
  97.7 0.8 fusion.6
  98.6 2.2 %multiply_reduce_fusion = f32[288,128]{1,0:T(8,128)} fusion(f32[16,128]{1,0:T(8,128)S(1)} %bitcast.21, f16[16,296,128]{2,1,0:T(8,128)(2,1)} %all-to-all-done), kind=kLoop, calls=%fused_computation.2 | loop fusion | flops 1732608 | bytes 1335296 | tf_op jit(solution)/shard_map/reduce_sum | solution.py:293
  (8 shorter events, 0.1 us)
Async XLA Ops:
  7.2 85.9 %reduce-scatter.2.cloned.1.call-start = ((), (), s32[]{:S(2)}) async-start(), calls=%async_computation.2 | async-start | bytes 5308416 | tf_op jit(solution)/shard_map/reduce_scatter | solution.py:276
  60.7 9.1 %collective-permute-start = (f32[8,288,128]{2,1,0:T(8,128)S(1)}, f32[8,288,128]{2,1,0:T(8,128)S(1)}, u32[]{:S(2)}, u32[]{:S(2)}) collective-permute-start(f32[8,288,128]{2,1,0:T(8,128)S(1)} %get-tuple-element.20), channel_id=1, source_target_pairs={{0,8},{8,0},{1,9},{9,1},{2,10},{10,2},{3,11},{11,3},{4,12},{12,4},... | collective-permute-start | bytes 3538952 | tf_op jit(solution)/shard_map/ppermute | solution.py:281
  67.1 3.0 %collective-permute-start.1 = (f32[8,288,128]{2,1,0:T(8,128)S(1)}, f32[8,288,128]{2,1,0:T(8,128)S(1)}, u32[]{:S(2)}, u32[]{:S(2)}) collective-permute-start(f32[8,288,128]{2,1,0:T(8,128)S(1)} %get-tuple-element.22), channel_id=1, source_target_pairs={{0,8},{8,0},{1,9},{9,1},{2,10},{10,2},{3,11},{11,3},{4,12},{12,4},... | collective-permute-start | bytes 3538952 | tf_op jit(solution)/shard_map/ppermute | solution.py:283
  70.5 8.7 %copy-start = (bf16[3,3,128,1024]{3,2,1,0:T(8,128)(2,1)S(1)}, bf16[3,3,128,1024]{3,2,1,0:T(8,128)(2,1)}, u32[]{:S(2)}) copy-start(bf16[3,3,128,1024]{3,2,1,0:T(8,128)(2,1)} %param.4) | copy-start | bytes 7077892
  70.5 8.7 %copy-start.1 = (bf16[512,1152]{1,0:T(8,128)(2,1)S(1)}, bf16[512,1152]{1,0:T(8,128)(2,1)}, u32[]{:S(2)}) copy-start(bf16[512,1152]{1,0:T(8,128)(2,1)} %get-tuple-element.27.refs_2_) | copy-start | bytes 3538948
  72.0 25.7 %all-to-all-start = ((f16[16,296,128]{2,1,0:T(8,128)(2,1)}), f16[16,296,128]{2,1,0:T(8,128)(2,1)}, u32[]{:S(2)}, u32[]{:S(2)}) async-start(f16[16,296,128]{2,1,0:T(8,128)(2,1)} %select_convert_fusion), calls=%async_computation | async-start | bytes 2424832 | tf_op jit(solution)/shard_map/all_to_all | solution.py:291
  79.2 1.1 copy-start.2
  80.3 1.1 copy-start.3
Sparse Core Ops, SparseCore 0:
  15.1 77.9 reduce-scatter.1
